TPU v7x, 1024 devices: a whole 4x4x32 slice. The times are simulated.
1024 devices in a mesh: expert: 64 (over z_lo, y), dp: 16 (over x, z_hi, core).
Axes of the slice: x: 4, y: 4, z: 32 (z_hi: 2, z_lo: 16; z = z_hi * 16 + z_lo), core: 2. Of those that a mesh axis runs over, the one named last changes fastest.
Arguments:
- tokens: bfloat16 [1024, 3584], P('expert', 'dp'), may hold values from -6 to 6
- expert_ids: int32 [1024, 8], P('expert'), may hold values from 0 to 63, all different within a row; in each aligned block of 16 rows (0 to 15, 16 to 31, ...) at most 4 rows name the same one
- route_weight: float32 [1024, 8], P('expert'), may hold values from 0.1 to 1
- swap_flags: int32 [32], replicated, may hold values from 0 to 1, as said below
- w_gate: bfloat16 [64, 1024, 3584], P('expert', None, 'dp'), may hold values from -0.09375 to 0.09375
- w_up: bfloat16 [64, 1024, 3584], P('expert', None, 'dp'), may hold values from -0.09375 to 0.09375
- w_down: bfloat16 [64, 1024, 3584], P('expert', None, 'dp'), may hold values from -0.1875 to 0.1875
- cotangent: bfloat16 [1024, 3584], P('expert', 'dp'), may hold values from -0.75 to 0.75
Outputs:
- mixed: bfloat16 [1024, 3584], P('expert', 'dp')
- input_grad: bfloat16 [1024, 3584], P('expert', 'dp')
- grad_gate: bfloat16 [64, 1024, 3584], P('expert', None, 'dp')
- grad_up: bfloat16 [64, 1024, 3584], P('expert', None, 'dp')
- grad_down: bfloat16 [64, 1024, 3584], P('expert', None, 'dp')
Inputs may be any that keep to these rules, and one draw needn't show every extreme that they name: `expert_ids`: in the 16 rows of one index of the expert axis (aligned blocks), each expert is named by at most 4 rows, a bound that some block reaches; a row names 8 different experts. `swap_flags`: entry p is 1 where slots p and p + 32 hold each other's experts; entry 0 is always 1, the others are 0 or 1.
All inputs are finite; a program needn't handle non-finite values.
Results may differ from a plain program's by a relative error of at most 0.0065.
Values may be sent and summed in bfloat16 or wider, within the bound.
No kernel may reach another device: no remote copies, remote signals or barrier semaphores. Data moves between devices by JAX's collectives and lax.ppermute only.
A program may use at most 32 MiB of HBM per device.

v0:
```python
import jax
import jax.numpy as jnp
from jax import lax
from jax.sharding import PartitionSpec as P


BF16 = jnp.bfloat16
F32 = jnp.float32
X_CHIPS, Z_HALVES, CORES = 4, 2, 2
Y_CHIPS = 4
PARTS = X_CHIPS * CORES


def exchanged(value, mask):
    size = lax.axis_size("dp")
    return lax.ppermute(value, "dp", [(i, i ^ mask) for i in range(size)])


def core_swap(value):
    return exchanged(value, 1)


def z_swap(value):
    return exchanged(value, CORES)


def x_swap(value, mask):
    return exchanged(value, mask * CORES * Z_HALVES)


def along_z(value, shift):
    experts, shards = lax.axis_size("expert"), lax.axis_size("dp")
    low = experts // Y_CHIPS
    pairs = []
    for expert in range(experts):
        place, y = divmod(expert, Y_CHIPS)
        for d in range(shards):
            x, half, core = d // 4, (d // 2) % 2, d % 2
            z = (half * low + place + shift) % (Z_HALVES * low)
            goal = (z % low) * Y_CHIPS + y
            pairs.append((expert * shards + d, goal * shards + x * 4 + (z // low) * 2 + core))
    return lax.ppermute(value, ("expert", "dp"), pairs)


def partner(value):
    experts = lax.axis_size("expert")
    return lax.ppermute(value, "expert", [(i, (i + experts // 2) % experts) for i in range(experts)])


def silu_parts(pre_gate):
    sigma = jax.nn.sigmoid(pre_gate)
    return (pre_gate * sigma, sigma * (1.0 + pre_gate * (1.0 - sigma)))


def matmul(left_side, right_side):
    return jnp.dot(left_side, right_side, preferred_element_type=F32)


def contract_first(left_side, right_side):
    return lax.dot_general(
        left_side, right_side, (((0,), (0,)), ((), ())), preferred_element_type=F32
    )


def contract_last(left_side, right_side):
    return lax.dot_general(
        left_side, right_side, (((1,), (1,)), ((), ())), preferred_element_type=F32
    )


def relative_blocks(rows, core, x):
    blocks = rows.reshape(2, 2, 2, rows.shape[0] // 8, rows.shape[1])
    for axis, bit in ((0, core), (1, x // 2), (2, x % 2)):
        blocks = jnp.where(bit == 1, jnp.flip(blocks, axis), blocks)
    return blocks.reshape(rows.shape)


def reduce_over_x(parts):
    total = parts[:, 0]
    for mask in range(1, X_CHIPS):
        total = total + x_swap(parts[:, mask].astype(BF16), mask).astype(F32)
    return total


def gather_over_x(mine):
    blocks = [mine]
    for mask in range(1, X_CHIPS):
        blocks.append(x_swap(mine, mask))
    return jnp.stack(blocks, axis=1)


def gather_all(mine):
    near = gather_over_x(mine)
    count, blocks, rows, width = near.shape
    near = near.reshape(count, blocks * rows, width)
    far = core_swap(near)
    return jnp.concatenate([near, far], axis=1)


def per_device(tokens, expert_ids, route_weight, swap_flags, w_gate, w_up, w_down, cotangent):
    experts = lax.axis_size("expert")
    half_axis = experts // 2
    my_index = lax.axis_index("expert")
    dp_index = lax.axis_index("dp")
    x, core = dp_index // 4, dp_index % 2
    tok_count, feat_width = tokens.shape
    top_count = expert_ids.shape[1]
    capacity = min(tok_count, max(2, 2 * tok_count * top_count // experts))
    slot_total = experts * capacity
    hidden_width = w_gate.shape[1]
    my_flag = lax.dynamic_index_in_dim(swap_flags, my_index % half_axis, keepdims=False)
    gate_w, up_w, down_w = (w[0].T for w in (w_gate, w_up, w_down))

    expert_rows = jnp.arange(experts, dtype=jnp.int32)
    named = expert_ids.T[None, :, :] == expert_rows[:, None, None]
    names = jnp.sum(named.astype(F32), axis=1)
    weights = jnp.sum(jnp.where(named, route_weight.T[None], 0.0), axis=1)
    before = jnp.arange(tok_count)[:, None] < jnp.arange(tok_count)[None, :]
    rank = matmul(names.astype(BF16), before.astype(BF16))
    ranks = jnp.arange(capacity, dtype=jnp.int32).astype(F32)
    placed = (names[:, None, :] > 0.5) & (rank[:, None, :] == ranks[None, :, None])
    placing = placed.astype(BF16).reshape(slot_total, tok_count)
    weighing = jnp.where(placed, weights[:, None, :], 0.0).reshape(slot_total, tok_count)
    slot_weight = jnp.sum(weighing, axis=1)

    def trade(outbound):
        moved = lax.all_to_all(
            outbound.reshape(experts, capacity, outbound.shape[1]),
            "expert",
            split_axis=0,
            concat_axis=0,
            tiled=True,
        )
        return moved.reshape(outbound.shape)

    spread = matmul(placing, jnp.concatenate([tokens, cotangent], axis=1))
    outbound = jnp.concatenate(
        [
            spread[:, :feat_width].astype(BF16),
            (slot_weight[:, None] * spread[:, feat_width:]).astype(BF16),
        ],
        axis=1,
    )
    arrived = trade(outbound)
    rows = relative_blocks(arrived, core, x)
    half_rows = slot_total // 2

    def partial_sums(some_rows):
        in_part, grad_part = some_rows[:, :feat_width], some_rows[:, feat_width:]
        return jnp.stack(
            [matmul(in_part, gate_w), matmul(in_part, up_w), matmul(grad_part, down_w)]
        )

    other_rows = core_swap(partial_sums(rows[half_rows:]))
    their_rows = partner(rows)
    sums = partial_sums(rows[:half_rows]) + other_rows
    sums = reduce_over_x(sums.reshape(3, X_CHIPS, slot_total // PARTS, hidden_width))
    sums = sums + z_swap(sums.astype(BF16)).astype(F32)
    pre_gate, up_value, hidden_grad = sums[0], sums[1], sums[2]
    activated, slope = silu_parts(pre_gate)
    factors = jnp.stack(
        [
            (activated * up_value).astype(BF16),
            (hidden_grad * up_value * slope).astype(BF16),
            (hidden_grad * activated).astype(BF16),
        ]
    )
    cut = factors.shape[1] // 2
    reach = experts // Y_CHIPS // 2
    first_cut = along_z(factors[:, :cut], reach)
    second_cut = along_z(factors[:, cut:], -reach)
    hidden, gate_grad, up_grad = gather_all(factors)
    expert_out = contract_last(hidden, down_w).astype(BF16)
    row_back = (contract_last(gate_grad, gate_w) + contract_last(up_grad, up_w)).astype(BF16)
    back = jnp.concatenate([expert_out, row_back], axis=1)
    first_cut, second_cut, _ = lax.optimization_barrier((first_cut, second_cut, back))
    theirs = jnp.concatenate([first_cut, second_cut], axis=1)
    held_factors = jnp.where(my_flag == 1, theirs, factors)
    returned = trade(relative_blocks(back, core, x))

    hidden, gate_grad, up_grad = gather_all(held_factors)
    held_rows = jnp.where(my_flag == 1, their_rows, rows)
    in_rows, grad_in = held_rows[:, :feat_width], held_rows[:, feat_width:]
    grads = (
        contract_first(gate_grad, in_rows).astype(BF16),
        contract_first(up_grad, in_rows).astype(BF16),
        contract_first(hidden, grad_in).astype(BF16),
    )

    mixed = lax.dot_general(
        weighing,
        returned[:, :feat_width].astype(F32),
        (((0,), (0,)), ((), ())),
        precision=lax.Precision.HIGHEST,
        preferred_element_type=F32,
    ).astype(BF16)
    input_grad = contract_first(placing, returned[:, feat_width:]).astype(BF16)
    return (mixed, input_grad, grads[0][None], grads[1][None], grads[2][None])


def solution(mesh):
    return jax.shard_map(
        per_device,
        mesh=mesh,
        in_specs=(
            P("expert", "dp"),
            P("expert", None),
            P("expert", None),
            P(),
            P("expert", None, "dp"),
            P("expert", None, "dp"),
            P("expert", None, "dp"),
            P("expert", "dp"),
        ),
        out_specs=(
            P("expert", "dp"),
            P("expert", "dp"),
            P("expert", None, "dp"),
            P("expert", None, "dp"),
            P("expert", None, "dp"),
        ),
        check_vma=False,
    )
```

profile of v0, /device:TPU:33, one launch (start us, length us, event | category | flops | bytes accessed | tf_op | source)
XLA Modules:
  0.0 305.4 jit_solution(15715705547814805545)
XLA Ops:
  4.6 28.5 %all-to-all-start = ((bf16[64,4,448]{2,1,0:T(4,128)(2,1)}), bf16[64,4,448]{2,1,0:T(4,128)(2,1)S(1)}, u32[]{:S(2)}, u32[]{:S(2)}) async-start(bf16[64,4,448]{2,1,0:T(4,128)(2,1)} %reshape.135), calls=%async_computation | async-start | bytes 524288 | tf_op jit(solution)/shard_map/all_to_all | solution.py:127
  33.2 32.4 %all-to-all-done = bf16[64,4,448]{2,1,0:T(4,128)(2,1)S(1)} async-done(((bf16[64,4,448]{2,1,0:T(4,128)(2,1)}), bf16[64,4,448]{2,1,0:T(4,128)(2,1)S(1)}, u32[]{:S(2)}, u32[]{:S(2)}) %all-to-all-start) | async-done | bytes 229408 | tf_op jit(solution)/shard_map/all_to_all | solution.py:127
  67.4 4.5 %collective-permute-start = (f32[3,128,1024]{2,1,0:T(8,128)S(1)}, f32[3,128,1024]{2,1,0:T(8,128)S(1)}, u32[]{:S(2)}, u32[]{:S(2)}) collective-permute-start(f32[3,128,1024]{2,1,0:T(8,128)S(1)} %pad_maximum_fusion), channel_id=1, source_target_pairs={{0,1},{1,0},{2,3},{3,2},{4,5},{5,4},{6,7},{7,6},{8,9},{9,8},{10,11... | collective-permute-start | bytes 4718600 | tf_op jit(solution)/shard_map/ppermute | solution.py:16
  72.7 2.3 collective-permute-done
  75.4 3.1 %collective-permute-start.1 = (bf16[3,32,1024]{2,1,0:T(8,128)(2,1)S(1)}, bf16[3,32,1024]{2,1,0:T(8,128)(2,1)S(1)}, u32[]{:S(2)}, u32[]{:S(2)}) collective-permute-start(bf16[3,32,1024]{2,1,0:T(8,128)(2,1)S(1)} %get-tuple-element.11), channel_id=1, source_target_pairs={{0,4},{1,5},{2,6},{3,7},{4,0},{5,1},{6,2},{7,3},{8,12},{9,13},{10,... | collective-permute-start | bytes 589832 | tf_op jit(solution)/shard_map/ppermute | solution.py:16
  78.5 4.4 %collective-permute-start.2 = (bf16[3,32,1024]{2,1,0:T(8,128)(2,1)S(1)}, bf16[3,32,1024]{2,1,0:T(8,128)(2,1)S(1)}, u32[]{:S(2)}, u32[]{:S(2)}) collective-permute-start(bf16[3,32,1024]{2,1,0:T(8,128)(2,1)S(1)} %get-tuple-element.13), channel_id=1, source_target_pairs={{0,8},{1,9},{2,10},{3,11},{4,12},{5,13},{6,14},{7,15},{8,0},{9,1},... | collective-permute-start | bytes 589832 | tf_op jit(solution)/shard_map/ppermute | solution.py:16
  85.0 4.8 %collective-permute-done.2 = bf16[3,32,1024]{2,1,0:T(8,128)(2,1)S(1)} collective-permute-done((bf16[3,32,1024]{2,1,0:T(8,128)(2,1)S(1)}, bf16[3,32,1024]{2,1,0:T(8,128)(2,1)S(1)}, u32[]{:S(2)}, u32[]{:S(2)}) %collective-permute-start.2) | collective-permute-done | bytes 196640 | tf_op jit(solution)/shard_map/ppermute | solution.py:16
  89.8 4.9 %collective-permute-done.3 = bf16[3,32,1024]{2,1,0:T(8,128)(2,1)S(1)} collective-permute-done((bf16[3,32,1024]{2,1,0:T(8,128)(2,1)S(1)}, bf16[3,32,1024]{2,1,0:T(8,128)(2,1)S(1)}, u32[]{:S(2)}, u32[]{:S(2)}) %collective-permute-start.3) | collective-permute-done | bytes 196640 | tf_op jit(solution)/shard_map/ppermute | solution.py:16
  94.9 11.6 %collective-permute-start.4 = (bf16[3,32,1024]{2,1,0:T(8,128)(2,1)S(1)}, bf16[3,32,1024]{2,1,0:T(8,128)(2,1)S(1)}, u32[]{:S(2)}, u32[]{:S(2)}) collective-permute-start(bf16[3,32,1024]{2,1,0:T(8,128)(2,1)S(1)} %fusion.55), channel_id=1, source_target_pairs={{0,2},{1,3},{2,0},{3,1},{4,6},{5,7},{6,4},{7,5},{8,10},{9,11},{10,... | collective-permute-start | bytes 589832 | tf_op jit(solution)/shard_map/ppermute | solution.py:16
  106.5 43.4 %collective-permute-done.4 = bf16[3,32,1024]{2,1,0:T(8,128)(2,1)S(1)} collective-permute-done((bf16[3,32,1024]{2,1,0:T(8,128)(2,1)S(1)}, bf16[3,32,1024]{2,1,0:T(8,128)(2,1)S(1)}, u32[]{:S(2)}, u32[]{:S(2)}) %collective-permute-start.4) | collective-permute-done | bytes 196640 | tf_op jit(solution)/shard_map/ppermute | solution.py:16
  152.0 3.3 %collective-permute-start.6 = (bf16[3,32,1024]{2,1,0:T(8,128)(2,1)S(1)}, bf16[3,32,1024]{2,1,0:T(8,128)(2,1)S(1)}, u32[]{:S(2)}, u32[]{:S(2)}) collective-permute-start(bf16[3,32,1024]{2,1,0:T(8,128)(2,1)S(1)} %get-tuple-element.22), channel_id=1, source_target_pairs={{0,8},{1,9},{2,10},{3,11},{4,12},{5,13},{6,14},{7,15},{8,0},{9,1},... | collective-permute-start | bytes 589832 | tf_op jit(solution)/shard_map/ppermute | solution.py:16
  155.3 4.4 %collective-permute-start.7 = (bf16[3,32,1024]{2,1,0:T(8,128)(2,1)S(1)}, bf16[3,32,1024]{2,1,0:T(8,128)(2,1)S(1)}, u32[]{:S(2)}, u32[]{:S(2)}) collective-permute-start(bf16[3,32,1024]{2,1,0:T(8,128)(2,1)S(1)} %get-tuple-element.22), channel_id=1, source_target_pairs={{0,12},{1,13},{2,14},{3,15},{4,8},{5,9},{6,10},{7,11},{8,4},{9,5},... | collective-permute-start | bytes 589832 | tf_op jit(solution)/shard_map/ppermute | solution.py:16
  159.7 2.6 collective-permute-done.6
  162.4 4.8 %collective-permute-done.7 = bf16[3,32,1024]{2,1,0:T(8,128)(2,1)S(1)} collective-permute-done((bf16[3,32,1024]{2,1,0:T(8,128)(2,1)S(1)}, bf16[3,32,1024]{2,1,0:T(8,128)(2,1)S(1)}, u32[]{:S(2)}, u32[]{:S(2)}) %collective-permute-start.7) | collective-permute-done | bytes 196640 | tf_op jit(solution)/shard_map/ppermute | solution.py:16
  167.3 2.4 collective-permute-start.8
  173.7 7.4 %all-to-all-start.1 = ((bf16[64,4,448]{2,1,0:T(4,128)(2,1)}), bf16[64,4,448]{2,1,0:T(4,128)(2,1)S(1)}, u32[]{:S(2)}, u32[]{:S(2)}) async-start(bf16[64,4,448]{2,1,0:T(4,128)(2,1)} %reshape_reshape.7), calls=%async_computation.1 | async-start | bytes 524288 | tf_op jit(solution)/shard_map/all_to_all | solution.py:127
  181.1 10.0 %collective-permute-start.10 = (bf16[3,16,1024]{2,1,0:T(8,128)(2,1)S(1)}, bf16[3,16,1024]{2,1,0:T(8,128)(2,1)S(1)}, u32[]{:S(2)}, u32[]{:S(2)}) collective-permute-start(bf16[3,16,1024]{2,1,0:T(8,128)(2,1)S(1)} %get-tuple-element.19), channel_id=1, source_target_pairs={{0,514},{1,515},{2,512},{3,513},{4,518},{5,519},{6,516},{7,517},{8... | collective-permute-start | bytes 294920 | tf_op jit(solution)/shard_map/ppermute | solution.py:42
  191.2 4.0 %collective-permute-start.9 = (bf16[3,16,1024]{2,1,0:T(8,128)(2,1)S(1)}, bf16[3,16,1024]{2,1,0:T(8,128)(2,1)S(1)}, u32[]{:S(2)}, u32[]{:S(2)}) collective-permute-start(bf16[3,16,1024]{2,1,0:T(8,128)(2,1)S(1)} %get-tuple-element.20), channel_id=1, source_target_pairs={{0,512},{1,513},{2,514},{3,515},{4,516},{5,517},{6,518},{7,519},{8... | collective-permute-start | bytes 294920 | tf_op jit(solution)/shard_map/ppermute | solution.py:42
  196.4 16.3 %collective-permute-done.10 = bf16[3,16,1024]{2,1,0:T(8,128)(2,1)S(1)} collective-permute-done((bf16[3,16,1024]{2,1,0:T(8,128)(2,1)S(1)}, bf16[3,16,1024]{2,1,0:T(8,128)(2,1)S(1)}, u32[]{:S(2)}, u32[]{:S(2)}) %collective-permute-start.10) | collective-permute-done | bytes 98336 | tf_op jit(solution)/shard_map/ppermute | solution.py:42
  212.8 2.4 collective-permute-start.11
  215.2 5.1 %collective-permute-start.12 = (bf16[3,32,1024]{2,1,0:T(8,128)(2,1)S(1)}, bf16[3,32,1024]{2,1,0:T(8,128)(2,1)S(1)}, u32[]{:S(2)}, u32[]{:S(2)}) collective-permute-start(bf16[3,32,1024]{2,1,0:T(8,128)(2,1)S(1)} %maximum_select_fusion.1), channel_id=1, source_target_pairs={{0,8},{1,9},{2,10},{3,11},{4,12},{5,13},{6,14},{7,15},{8,0},{9,1},... | collective-permute-start | bytes 589832 | tf_op jit(solution)/shard_map/ppermute | solution.py:16
  223.8 4.4 %collective-permute-done.13 = bf16[3,32,1024]{2,1,0:T(8,128)(2,1)S(1)} collective-permute-done((bf16[3,32,1024]{2,1,0:T(8,128)(2,1)S(1)}, bf16[3,32,1024]{2,1,0:T(8,128)(2,1)S(1)}, u32[]{:S(2)}, u32[]{:S(2)}) %collective-permute-start.13) | collective-permute-done | bytes 196640 | tf_op jit(solution)/shard_map/ppermute | solution.py:16
  228.4 22.2 %collective-permute-start.14 = (bf16[3,128,1024]{2,1,0:T(8,128)(2,1)S(1)}, bf16[3,128,1024]{2,1,0:T(8,128)(2,1)S(1)}, u32[]{:S(2)}, u32[]{:S(2)}) collective-permute-start(bf16[3,128,1024]{2,1,0:T(8,128)(2,1)S(1)} %bitcast.116), channel_id=1, source_target_pairs={{0,1},{1,0},{2,3},{3,2},{4,5},{5,4},{6,7},{7,6},{8,9},{9,8},{10,11... | collective-permute-start | bytes 2359304 | tf_op jit(solution)/shard_map/ppermute | solution.py:16
  252.5 47.6 %collective-permute-done.15 = bf16[256,448]{1,0:T(8,128)(2,1)S(1)} collective-permute-done((bf16[256,448]{1,0:T(8,128)(2,1)S(1)}, bf16[256,448]{1,0:T(8,128)(2,1)S(1)}, u32[]{:S(2)}, u32[]{:S(2)}) %collective-permute-start.15) | collective-permute-done | bytes 229408 | tf_op jit(solution)/shard_map/ppermute | solution.py:47
  (81 shorter events, 26.7 us)
Async XLA Ops:
  0.6 65.3 %copy-start = (bf16[1,1024,224]{1,2,0:T(8,128)(2,1)S(1)}, bf16[1,1024,224]{1,2,0:T(8,128)(2,1)}, u32[]{:S(2)}) copy-start(bf16[1,1024,224]{1,2,0:T(8,128)(2,1)} %param.14) | copy-start | bytes 1376260
  4.6 61.0 %all-to-all-start = ((bf16[64,4,448]{2,1,0:T(4,128)(2,1)}), bf16[64,4,448]{2,1,0:T(4,128)(2,1)S(1)}, u32[]{:S(2)}, u32[]{:S(2)}) async-start(bf16[64,4,448]{2,1,0:T(4,128)(2,1)} %reshape.135), calls=%async_computation | async-start | bytes 524288 | tf_op jit(solution)/shard_map/all_to_all | solution.py:127
  65.7 1.0 copy-start.2
  65.9 1.1 copy-start.1
  67.4 7.6 %collective-permute-start = (f32[3,128,1024]{2,1,0:T(8,128)S(1)}, f32[3,128,1024]{2,1,0:T(8,128)S(1)}, u32[]{:S(2)}, u32[]{:S(2)}) collective-permute-start(f32[3,128,1024]{2,1,0:T(8,128)S(1)} %pad_maximum_fusion), channel_id=1, source_target_pairs={{0,1},{1,0},{2,3},{3,2},{4,5},{5,4},{6,7},{7,6},{8,9},{9,8},{10,11... | collective-permute-start | bytes 4718600 | tf_op jit(solution)/shard_map/ppermute | solution.py:16
  75.4 9.6 %collective-permute-start.1 = (bf16[3,32,1024]{2,1,0:T(8,128)(2,1)S(1)}, bf16[3,32,1024]{2,1,0:T(8,128)(2,1)S(1)}, u32[]{:S(2)}, u32[]{:S(2)}) collective-permute-start(bf16[3,32,1024]{2,1,0:T(8,128)(2,1)S(1)} %get-tuple-element.11), channel_id=1, source_target_pairs={{0,4},{1,5},{2,6},{3,7},{4,0},{5,1},{6,2},{7,3},{8,12},{9,13},{10,... | collective-permute-start | bytes 589832 | tf_op jit(solution)/shard_map/ppermute | solution.py:16
  78.5 11.3 %collective-permute-start.2 = (bf16[3,32,1024]{2,1,0:T(8,128)(2,1)S(1)}, bf16[3,32,1024]{2,1,0:T(8,128)(2,1)S(1)}, u32[]{:S(2)}, u32[]{:S(2)}) collective-permute-start(bf16[3,32,1024]{2,1,0:T(8,128)(2,1)S(1)} %get-tuple-element.13), channel_id=1, source_target_pairs={{0,8},{1,9},{2,10},{3,11},{4,12},{5,13},{6,14},{7,15},{8,0},{9,1},... | collective-permute-start | bytes 589832 | tf_op jit(solution)/shard_map/ppermute | solution.py:16
  82.9 11.8 %collective-permute-start.3 = (bf16[3,32,1024]{2,1,0:T(8,128)(2,1)S(1)}, bf16[3,32,1024]{2,1,0:T(8,128)(2,1)S(1)}, u32[]{:S(2)}, u32[]{:S(2)}) collective-permute-start(bf16[3,32,1024]{2,1,0:T(8,128)(2,1)S(1)} %get-tuple-element.12), channel_id=1, source_target_pairs={{0,12},{1,13},{2,14},{3,15},{4,8},{5,9},{6,10},{7,11},{8,4},{9,5},... | collective-permute-start | bytes 589832 | tf_op jit(solution)/shard_map/ppermute | solution.py:16
  94.9 55.0 %collective-permute-start.4 = (bf16[3,32,1024]{2,1,0:T(8,128)(2,1)S(1)}, bf16[3,32,1024]{2,1,0:T(8,128)(2,1)S(1)}, u32[]{:S(2)}, u32[]{:S(2)}) collective-permute-start(bf16[3,32,1024]{2,1,0:T(8,128)(2,1)S(1)} %fusion.55), channel_id=1, source_target_pairs={{0,2},{1,3},{2,0},{3,1},{4,6},{5,7},{6,4},{7,5},{8,10},{9,11},{10,... | collective-permute-start | bytes 589832 | tf_op jit(solution)/shard_map/ppermute | solution.py:16
  150.1 9.6 %collective-permute-start.5 = (bf16[3,32,1024]{2,1,0:T(8,128)(2,1)S(1)}, bf16[3,32,1024]{2,1,0:T(8,128)(2,1)S(1)}, u32[]{:S(2)}, u32[]{:S(2)}) collective-permute-start(bf16[3,32,1024]{2,1,0:T(8,128)(2,1)S(1)} %get-tuple-element.22), channel_id=1, source_target_pairs={{0,4},{1,5},{2,6},{3,7},{4,0},{5,1},{6,2},{7,3},{8,12},{9,13},{10,... | collective-permute-start | bytes 589832 | tf_op jit(solution)/shard_map/ppermute | solution.py:16
  152.0 10.3 %collective-permute-start.6 = (bf16[3,32,1024]{2,1,0:T(8,128)(2,1)S(1)}, bf16[3,32,1024]{2,1,0:T(8,128)(2,1)S(1)}, u32[]{:S(2)}, u32[]{:S(2)}) collective-permute-start(bf16[3,32,1024]{2,1,0:T(8,128)(2,1)S(1)} %get-tuple-element.22), channel_id=1, source_target_pairs={{0,8},{1,9},{2,10},{3,11},{4,12},{5,13},{6,14},{7,15},{8,0},{9,1},... | collective-permute-start | bytes 589832 | tf_op jit(solution)/shard_map/ppermute | solution.py:16
  155.3 11.8 %collective-permute-start.7 = (bf16[3,32,1024]{2,1,0:T(8,128)(2,1)S(1)}, bf16[3,32,1024]{2,1,0:T(8,128)(2,1)S(1)}, u32[]{:S(2)}, u32[]{:S(2)}) collective-permute-start(bf16[3,32,1024]{2,1,0:T(8,128)(2,1)S(1)} %get-tuple-element.22), channel_id=1, source_target_pairs={{0,12},{1,13},{2,14},{3,15},{4,8},{5,9},{6,10},{7,11},{8,4},{9,5},... | collective-permute-start | bytes 589832 | tf_op jit(solution)/shard_map/ppermute | solution.py:16
  167.3 4.3 %collective-permute-start.8 = (bf16[3,128,1024]{2,1,0:T(8,128)(2,1)S(1)}, bf16[3,128,1024]{2,1,0:T(8,128)(2,1)S(1)}, u32[]{:S(2)}, u32[]{:S(2)}) collective-permute-start(bf16[3,128,1024]{2,1,0:T(8,128)(2,1)S(1)} %bitcast.120), channel_id=1, source_target_pairs={{0,1},{1,0},{2,3},{3,2},{4,5},{5,4},{6,7},{7,6},{8,9},{9,8},{10,11... | collective-permute-start | bytes 2359304 | tf_op jit(solution)/shard_map/ppermute | solution.py:16
  172.8 22.4 %copy-start.3 = (s32[32]{0:T(128)S(1)}, s32[32]{0:T(128)}, u32[]{:S(2)}) copy-start(s32[32]{0:T(128)} %param.11) | copy-start | bytes 388
  173.7 129.8 %all-to-all-start.1 = ((bf16[64,4,448]{2,1,0:T(4,128)(2,1)}), bf16[64,4,448]{2,1,0:T(4,128)(2,1)S(1)}, u32[]{:S(2)}, u32[]{:S(2)}) async-start(bf16[64,4,448]{2,1,0:T(4,128)(2,1)} %reshape_reshape.7), calls=%async_computation.1 | async-start | bytes 524288 | tf_op jit(solution)/shard_map/all_to_all | solution.py:127
  181.1 31.6 %collective-permute-start.10 = (bf16[3,16,1024]{2,1,0:T(8,128)(2,1)S(1)}, bf16[3,16,1024]{2,1,0:T(8,128)(2,1)S(1)}, u32[]{:S(2)}, u32[]{:S(2)}) collective-permute-start(bf16[3,16,1024]{2,1,0:T(8,128)(2,1)S(1)} %get-tuple-element.19), channel_id=1, source_target_pairs={{0,514},{1,515},{2,512},{3,513},{4,518},{5,519},{6,516},{7,517},{8... | collective-permute-start | bytes 294920 | tf_op jit(solution)/shard_map/ppermute | solution.py:42
  191.2 21.6 %collective-permute-start.9 = (bf16[3,16,1024]{2,1,0:T(8,128)(2,1)S(1)}, bf16[3,16,1024]{2,1,0:T(8,128)(2,1)S(1)}, u32[]{:S(2)}, u32[]{:S(2)}) collective-permute-start(bf16[3,16,1024]{2,1,0:T(8,128)(2,1)S(1)} %get-tuple-element.20), channel_id=1, source_target_pairs={{0,512},{1,513},{2,514},{3,515},{4,516},{5,517},{6,518},{7,519},{8... | collective-permute-start | bytes 294920 | tf_op jit(solution)/shard_map/ppermute | solution.py:42
  212.8 9.7 %collective-permute-start.11 = (bf16[3,32,1024]{2,1,0:T(8,128)(2,1)S(1)}, bf16[3,32,1024]{2,1,0:T(8,128)(2,1)S(1)}, u32[]{:S(2)}, u32[]{:S(2)}) collective-permute-start(bf16[3,32,1024]{2,1,0:T(8,128)(2,1)S(1)} %maximum_select_fusion.1), channel_id=1, source_target_pairs={{0,4},{1,5},{2,6},{3,7},{4,0},{5,1},{6,2},{7,3},{8,12},{9,13},{10,... | collective-permute-start | bytes 589832 | tf_op jit(solution)/shard_map/ppermute | solution.py:16
  215.2 8.6 %collective-permute-start.12 = (bf16[3,32,1024]{2,1,0:T(8,128)(2,1)S(1)}, bf16[3,32,1024]{2,1,0:T(8,128)(2,1)S(1)}, u32[]{:S(2)}, u32[]{:S(2)}) collective-permute-start(bf16[3,32,1024]{2,1,0:T(8,128)(2,1)S(1)} %maximum_select_fusion.1), channel_id=1, source_target_pairs={{0,8},{1,9},{2,10},{3,11},{4,12},{5,13},{6,14},{7,15},{8,0},{9,1},... | collective-permute-start | bytes 589832 | tf_op jit(solution)/shard_map/ppermute | solution.py:16
  220.3 7.9 %collective-permute-start.13 = (bf16[3,32,1024]{2,1,0:T(8,128)(2,1)S(1)}, bf16[3,32,1024]{2,1,0:T(8,128)(2,1)S(1)}, u32[]{:S(2)}, u32[]{:S(2)}) collective-permute-start(bf16[3,32,1024]{2,1,0:T(8,128)(2,1)S(1)} %maximum_select_fusion.1), channel_id=1, source_target_pairs={{0,12},{1,13},{2,14},{3,15},{4,8},{5,9},{6,10},{7,11},{8,4},{9,5},... | collective-permute-start | bytes 589832 | tf_op jit(solution)/shard_map/ppermute | solution.py:16
  228.4 71.8 %collective-permute-start.14 = (bf16[3,128,1024]{2,1,0:T(8,128)(2,1)S(1)}, bf16[3,128,1024]{2,1,0:T(8,128)(2,1)S(1)}, u32[]{:S(2)}, u32[]{:S(2)}) collective-permute-start(bf16[3,128,1024]{2,1,0:T(8,128)(2,1)S(1)} %bitcast.116), channel_id=1, source_target_pairs={{0,1},{1,0},{2,3},{3,2},{4,5},{5,4},{6,7},{7,6},{8,9},{9,8},{10,11... | collective-permute-start | bytes 2359304 | tf_op jit(solution)/shard_map/ppermute | solution.py:16
  250.5 49.6 %collective-permute-start.15 = (bf16[256,448]{1,0:T(8,128)(2,1)S(1)}, bf16[256,448]{1,0:T(8,128)(2,1)S(1)}, u32[]{:S(2)}, u32[]{:S(2)}) collective-permute-start(bf16[256,448]{1,0:T(8,128)(2,1)S(1)} %bitcast.127), channel_id=1, source_target_pairs={{0,512},{16,528},{32,544},{48,560},{64,576},{80,592},{96,608},{112... | collective-permute-start | bytes 688136 | tf_op jit(solution)/shard_map/ppermute | solution.py:47
where the time goes:
time: 306 us; the launch traced here: 305 us
  waiting for transfers between devices  167 us (55%)
  starting transfers between devices  121 us (40%)
  matrix products  8.74 us (3%)
  local copies, waits for them, and re-layouts  3.87 us (1%)
    ppermute x13, waiting for transfers between devices, exchanged(): return lax.ppermute(value, 'dp', [(i, i ^ mask) for i in range(size)])  70.5 us
    ppermute x13, starting transfers between devices, exchanged(): return lax.ppermute(value, 'dp', [(i, i ^ mask) for i in range(size)])  69.4 us
    ppermute x1, waiting for transfers between devices, partner(): lax.ppermute(value, 'expert', [(i, (i + experts // 2) % experts) for i in...  47.6 us
    all_to_all x2, starting transfers between devices, trade(): lax.all_to_all(outbound.reshape(experts, capacity, outbound.shape[1]), 'e...  35.9 us
    all_to_all x2, waiting for transfers between devices, trade(): lax.all_to_all(outbound.reshape(experts, capacity, outbound.shape[1]), 'e...  32.4 us
    ppermute x2, waiting for transfers between devices, along_z(): return lax.ppermute(value, ('expert', 'dp'), pairs)  16.3 us
    ppermute x2, starting transfers between devices, along_z(): return lax.ppermute(value, ('expert', 'dp'), pairs)  14 us
  transfers between devices with their start and end apart: 18, of which 12 were waited for; matrix products, arithmetic and copies ran while one was open for 2% of the time, Pallas kernels for 0%

commit v1 on v0

--- a/solution.py
+++ b/solution.py
@@ -40,11 +40,6 @@
             goal = (z % low) * Y_CHIPS + y
             pairs.append((expert * shards + d, goal * shards + x * 4 + (z // low) * 2 + core))
     return lax.ppermute(value, ("expert", "dp"), pairs)
-
-
-def partner(value):
-    experts = lax.axis_size("expert")
-    return lax.ppermute(value, "expert", [(i, (i + experts // 2) % experts) for i in range(experts)])
 
 
 def silu_parts(pre_gate):
@@ -111,17 +106,29 @@
     my_flag = lax.dynamic_index_in_dim(swap_flags, my_index % half_axis, keepdims=False)
     gate_w, up_w, down_w = (w[0].T for w in (w_gate, w_up, w_down))
 
-    expert_rows = jnp.arange(experts, dtype=jnp.int32)
-    named = expert_ids.T[None, :, :] == expert_rows[:, None, None]
-    names = jnp.sum(named.astype(F32), axis=1)
-    weights = jnp.sum(jnp.where(named, route_weight.T[None], 0.0), axis=1)
-    before = jnp.arange(tok_count)[:, None] < jnp.arange(tok_count)[None, :]
-    rank = matmul(names.astype(BF16), before.astype(BF16))
+    before = (jnp.arange(tok_count)[:, None] < jnp.arange(tok_count)[None, :]).astype(BF16)
     ranks = jnp.arange(capacity, dtype=jnp.int32).astype(F32)
-    placed = (names[:, None, :] > 0.5) & (rank[:, None, :] == ranks[None, :, None])
-    placing = placed.astype(BF16).reshape(slot_total, tok_count)
-    weighing = jnp.where(placed, weights[:, None, :], 0.0).reshape(slot_total, tok_count)
-    slot_weight = jnp.sum(weighing, axis=1)
+
+    def slots_of(some_experts):
+        named = expert_ids.T[None, :, :] == some_experts[:, None, None]
+        names = jnp.sum(named.astype(F32), axis=1)
+        weights = jnp.sum(jnp.where(named, route_weight.T[None], 0.0), axis=1)
+        rank = matmul(names.astype(BF16), before)
+        placed = (names[:, None, :] > 0.5) & (rank[:, None, :] == ranks[None, :, None])
+        placing = placed.astype(BF16).reshape(slot_total, tok_count)
+        weighing = jnp.where(placed, weights[:, None, :], 0.0).reshape(slot_total, tok_count)
+        return placing, weighing
+
+    def packed(placing, weighing):
+        slot_weight = jnp.sum(weighing, axis=1)
+        scaled = slot_weight[:, None] * matmul(placing, cotangent)
+        return matmul(placing, tokens).astype(BF16), scaled.astype(BF16)
+
+    slots = jnp.arange(experts, dtype=jnp.int32)
+    holds = jnp.where(jnp.tile(swap_flags, 2) == 1, (slots + half_axis) % experts, slots)
+    placing, weighing = slots_of(slots)
+    outbound = jnp.concatenate([*packed(placing, weighing), *packed(*slots_of(holds))], axis=1)
+    width = 2 * feat_width
 
     def trade(outbound):
         moved = lax.all_to_all(
@@ -133,16 +140,9 @@
         )
         return moved.reshape(outbound.shape)
 
-    spread = matmul(placing, jnp.concatenate([tokens, cotangent], axis=1))
-    outbound = jnp.concatenate(
-        [
-            spread[:, :feat_width].astype(BF16),
-            (slot_weight[:, None] * spread[:, feat_width:]).astype(BF16),
-        ],
-        axis=1,
-    )
     arrived = trade(outbound)
-    rows = relative_blocks(arrived, core, x)
+    arrived = relative_blocks(arrived, core, x)
+    rows, held_rows = arrived[:, :width], arrived[:, width:]
     half_rows = slot_total // 2
 
     def partial_sums(some_rows):
@@ -152,7 +152,6 @@
         )
 
     other_rows = core_swap(partial_sums(rows[half_rows:]))
-    their_rows = partner(rows)
     sums = partial_sums(rows[:half_rows]) + other_rows
     sums = reduce_over_x(sums.reshape(3, X_CHIPS, slot_total // PARTS, hidden_width))
     sums = sums + z_swap(sums.astype(BF16)).astype(F32)
@@ -179,7 +178,6 @@
     returned = trade(relative_blocks(back, core, x))
 
     hidden, gate_grad, up_grad = gather_all(held_factors)
-    held_rows = jnp.where(my_flag == 1, their_rows, rows)
     in_rows, grad_in = held_rows[:, :feat_width], held_rows[:, feat_width:]
     grads = (
         contract_first(gate_grad, in_rows).astype(BF16),

time: 306 us -> 281 us (0.918)
  waiting for transfers between devices: 167 us -> 131 us
  starting transfers between devices: 121 us -> 129 us
    ppermute x1 -> x0, waiting for transfers between devices: 47.6 us -> none  [partner(): lax.ppermute(value, 'expert', [(i, (i + experts // 2) % experts) for i in...]
    all_to_all x2, waiting for transfers between devices: 32.4 us -> 46.4 us  [trade(): lax.all_to_all(outbound.reshape(experts, capacity, outbound.shape[1]), 'e...]
    all_to_all x2, starting transfers between devices: 35.9 us -> 43.3 us  [trade(): lax.all_to_all(outbound.reshape(experts, capacity, outbound.shape[1]), 'e...]
  transfers between devices with their start and end apart: 18 -> 17, of which waited for: 12 -> 12; matrix products, arithmetic and copies ran while one was open for 2% -> 2% of each run, Pallas kernels for 0% -> 0%
where the time goes in v1:
time: 281 us; the launch traced here: 280 us
  waiting for transfers between devices  131 us (47%)
  starting transfers between devices  129 us (46%)
  matrix products  9.63 us (3%)
  local copies, waits for them, and re-layouts  4.51 us (2%)
  other arithmetic  3.57 us (1%)
    ppermute x13, starting transfers between devices, exchanged(): return lax.ppermute(value, 'dp', [(i, i ^ mask) for i in range(size)])  71.8 us
    ppermute x13, waiting for transfers between devices, exchanged(): return lax.ppermute(value, 'dp', [(i, i ^ mask) for i in range(size)])  68 us
    all_to_all x2, waiting for transfers between devices, trade(): lax.all_to_all(outbound.reshape(experts, capacity, outbound.shape[1]), 'e...  46.4 us
    all_to_all x2, starting transfers between devices, trade(): lax.all_to_all(outbound.reshape(experts, capacity, outbound.shape[1]), 'e...  43.3 us
    ppermute x2, waiting for transfers between devices, along_z(): return lax.ppermute(value, ('expert', 'dp'), pairs)  17.1 us
    ppermute x2, starting transfers between devices, along_z(): return lax.ppermute(value, ('expert', 'dp'), pairs)  14 us
  transfers between devices with their start and end apart: 17, of which 12 were waited for; matrix products, arithmetic and copies ran while one was open for 2% of the time, Pallas kernels for 0%

profile of v1, /device:TPU:33, one launch (start us, length us, event | category | flops | bytes accessed | tf_op | source)
XLA Modules:
  0.0 280.2 jit_solution(15580630251316747425)
XLA Ops:
  6.8 28.5 %all-to-all-start = ((bf16[64,4,896]{2,1,0:T(4,128)(2,1)}), bf16[64,4,896]{2,1,0:T(4,128)(2,1)S(1)}, u32[]{:S(2)}, u32[]{:S(2)}) async-start(bf16[64,4,896]{2,1,0:T(4,128)(2,1)} %reshape.181), calls=%async_computation | async-start | bytes 917504 | tf_op jit(solution)/shard_map/all_to_all | solution.py:134
  35.4 46.4 %all-to-all-done = bf16[64,4,896]{2,1,0:T(4,128)(2,1)S(1)} async-done(((bf16[64,4,896]{2,1,0:T(4,128)(2,1)}), bf16[64,4,896]{2,1,0:T(4,128)(2,1)S(1)}, u32[]{:S(2)}, u32[]{:S(2)}) %all-to-all-start) | async-done | bytes 458784 | tf_op jit(solution)/shard_map/all_to_all | solution.py:134
  83.6 7.7 %collective-permute-start = (f32[3,128,1024]{2,1,0:T(8,128)S(1)}, f32[3,128,1024]{2,1,0:T(8,128)S(1)}, u32[]{:S(2)}, u32[]{:S(2)}) collective-permute-start(f32[3,128,1024]{2,1,0:T(8,128)S(1)} %pad_maximum_fusion), channel_id=1, source_target_pairs={{0,1},{1,0},{2,3},{3,2},{4,5},{5,4},{6,7},{7,6},{8,9},{9,8},{10,11... | collective-permute-start | bytes 4718600 | tf_op jit(solution)/shard_map/ppermute | solution.py:16
  92.0 2.3 collective-permute-done
  94.8 3.1 %collective-permute-start.1 = (bf16[3,32,1024]{2,1,0:T(8,128)(2,1)S(1)}, bf16[3,32,1024]{2,1,0:T(8,128)(2,1)S(1)}, u32[]{:S(2)}, u32[]{:S(2)}) collective-permute-start(bf16[3,32,1024]{2,1,0:T(8,128)(2,1)S(1)} %get-tuple-element.15), channel_id=1, source_target_pairs={{0,4},{1,5},{2,6},{3,7},{4,0},{5,1},{6,2},{7,3},{8,12},{9,13},{10,... | collective-permute-start | bytes 589832 | tf_op jit(solution)/shard_map/ppermute | solution.py:16
  97.9 4.4 %collective-permute-start.2 = (bf16[3,32,1024]{2,1,0:T(8,128)(2,1)S(1)}, bf16[3,32,1024]{2,1,0:T(8,128)(2,1)S(1)}, u32[]{:S(2)}, u32[]{:S(2)}) collective-permute-start(bf16[3,32,1024]{2,1,0:T(8,128)(2,1)S(1)} %get-tuple-element.17), channel_id=1, source_target_pairs={{0,8},{1,9},{2,10},{3,11},{4,12},{5,13},{6,14},{7,15},{8,0},{9,1},... | collective-permute-start | bytes 589832 | tf_op jit(solution)/shard_map/ppermute | solution.py:16
  104.4 4.8 %collective-permute-done.2 = bf16[3,32,1024]{2,1,0:T(8,128)(2,1)S(1)} collective-permute-done((bf16[3,32,1024]{2,1,0:T(8,128)(2,1)S(1)}, bf16[3,32,1024]{2,1,0:T(8,128)(2,1)S(1)}, u32[]{:S(2)}, u32[]{:S(2)}) %collective-permute-start.2) | collective-permute-done | bytes 196640 | tf_op jit(solution)/shard_map/ppermute | solution.py:16
  109.2 4.9 %collective-permute-done.3 = bf16[3,32,1024]{2,1,0:T(8,128)(2,1)S(1)} collective-permute-done((bf16[3,32,1024]{2,1,0:T(8,128)(2,1)S(1)}, bf16[3,32,1024]{2,1,0:T(8,128)(2,1)S(1)}, u32[]{:S(2)}, u32[]{:S(2)}) %collective-permute-start.3) | collective-permute-done | bytes 196640 | tf_op jit(solution)/shard_map/ppermute | solution.py:16
  114.2 11.6 %collective-permute-start.4 = (bf16[3,32,1024]{2,1,0:T(8,128)(2,1)S(1)}, bf16[3,32,1024]{2,1,0:T(8,128)(2,1)S(1)}, u32[]{:S(2)}, u32[]{:S(2)}) collective-permute-start(bf16[3,32,1024]{2,1,0:T(8,128)(2,1)S(1)} %fusion.55), channel_id=1, source_target_pairs={{0,2},{1,3},{2,0},{3,1},{4,6},{5,7},{6,4},{7,5},{8,10},{9,11},{10,... | collective-permute-start | bytes 589832 | tf_op jit(solution)/shard_map/ppermute | solution.py:16
  125.8 39.1 %collective-permute-done.4 = bf16[3,32,1024]{2,1,0:T(8,128)(2,1)S(1)} collective-permute-done((bf16[3,32,1024]{2,1,0:T(8,128)(2,1)S(1)}, bf16[3,32,1024]{2,1,0:T(8,128)(2,1)S(1)}, u32[]{:S(2)}, u32[]{:S(2)}) %collective-permute-start.4) | collective-permute-done | bytes 196640 | tf_op jit(solution)/shard_map/ppermute | solution.py:16
  167.1 3.3 %collective-permute-start.6 = (bf16[3,32,1024]{2,1,0:T(8,128)(2,1)S(1)}, bf16[3,32,1024]{2,1,0:T(8,128)(2,1)S(1)}, u32[]{:S(2)}, u32[]{:S(2)}) collective-permute-start(bf16[3,32,1024]{2,1,0:T(8,128)(2,1)S(1)} %get-tuple-element.24), channel_id=1, source_target_pairs={{0,8},{1,9},{2,10},{3,11},{4,12},{5,13},{6,14},{7,15},{8,0},{9,1},... | collective-permute-start | bytes 589832 | tf_op jit(solution)/shard_map/ppermute | solution.py:16
  170.4 4.4 %collective-permute-start.7 = (bf16[3,32,1024]{2,1,0:T(8,128)(2,1)S(1)}, bf16[3,32,1024]{2,1,0:T(8,128)(2,1)S(1)}, u32[]{:S(2)}, u32[]{:S(2)}) collective-permute-start(bf16[3,32,1024]{2,1,0:T(8,128)(2,1)S(1)} %get-tuple-element.24), channel_id=1, source_target_pairs={{0,12},{1,13},{2,14},{3,15},{4,8},{5,9},{6,10},{7,11},{8,4},{9,5},... | collective-permute-start | bytes 589832 | tf_op jit(solution)/shard_map/ppermute | solution.py:16
  174.8 2.6 collective-permute-done.6
  177.4 4.8 %collective-permute-done.7 = bf16[3,32,1024]{2,1,0:T(8,128)(2,1)S(1)} collective-permute-done((bf16[3,32,1024]{2,1,0:T(8,128)(2,1)S(1)}, bf16[3,32,1024]{2,1,0:T(8,128)(2,1)S(1)}, u32[]{:S(2)}, u32[]{:S(2)}) %collective-permute-start.7) | collective-permute-done | bytes 196640 | tf_op jit(solution)/shard_map/ppermute | solution.py:16
  182.3 2.4 collective-permute-start.8
  188.8 14.8 %all-to-all-start.1 = ((bf16[64,4,448]{2,1,0:T(4,128)(2,1)}), bf16[64,4,448]{2,1,0:T(4,128)(2,1)S(1)}, u32[]{:S(2)}, u32[]{:S(2)}) async-start(bf16[64,4,448]{2,1,0:T(4,128)(2,1)} %reshape_reshape.7), calls=%async_computation.1 | async-start | bytes 524288 | tf_op jit(solution)/shard_map/all_to_all | solution.py:134
  203.6 11.2 %collective-permute-start.10 = (bf16[3,16,1024]{2,1,0:T(8,128)(2,1)S(1)}, bf16[3,16,1024]{2,1,0:T(8,128)(2,1)S(1)}, u32[]{:S(2)}, u32[]{:S(2)}) collective-permute-start(bf16[3,16,1024]{2,1,0:T(8,128)(2,1)S(1)} %get-tuple-element.21), channel_id=1, source_target_pairs={{0,514},{1,515},{2,512},{3,513},{4,518},{5,519},{6,516},{7,517},{8... | collective-permute-start | bytes 294920 | tf_op jit(solution)/shard_map/ppermute | solution.py:42
  214.8 2.7 collective-permute-start.9
  218.8 17.1 %collective-permute-done.10 = bf16[3,16,1024]{2,1,0:T(8,128)(2,1)S(1)} collective-permute-done((bf16[3,16,1024]{2,1,0:T(8,128)(2,1)S(1)}, bf16[3,16,1024]{2,1,0:T(8,128)(2,1)S(1)}, u32[]{:S(2)}, u32[]{:S(2)}) %collective-permute-start.10) | collective-permute-done | bytes 98336 | tf_op jit(solution)/shard_map/ppermute | solution.py:42
  236.0 2.7 collective-permute-start.11
  238.7 4.8 %collective-permute-start.12 = (bf16[3,32,1024]{2,1,0:T(8,128)(2,1)S(1)}, bf16[3,32,1024]{2,1,0:T(8,128)(2,1)S(1)}, u32[]{:S(2)}, u32[]{:S(2)}) collective-permute-start(bf16[3,32,1024]{2,1,0:T(8,128)(2,1)S(1)} %maximum_select_fusion.1), channel_id=1, source_target_pairs={{0,8},{1,9},{2,10},{3,11},{4,12},{5,13},{6,14},{7,15},{8,0},{9,1},... | collective-permute-start | bytes 589832 | tf_op jit(solution)/shard_map/ppermute | solution.py:16
  243.5 2.1 collective-permute-start.13
  247.0 4.4 %collective-permute-done.13 = bf16[3,32,1024]{2,1,0:T(8,128)(2,1)S(1)} collective-permute-done((bf16[3,32,1024]{2,1,0:T(8,128)(2,1)S(1)}, bf16[3,32,1024]{2,1,0:T(8,128)(2,1)S(1)}, u32[]{:S(2)}, u32[]{:S(2)}) %collective-permute-start.13) | collective-permute-done | bytes 196640 | tf_op jit(solution)/shard_map/ppermute | solution.py:16
  251.6 21.4 %collective-permute-start.14 = (bf16[3,128,1024]{2,1,0:T(8,128)(2,1)S(1)}, bf16[3,128,1024]{2,1,0:T(8,128)(2,1)S(1)}, u32[]{:S(2)}, u32[]{:S(2)}) collective-permute-start(bf16[3,128,1024]{2,1,0:T(8,128)(2,1)S(1)} %bitcast.126), channel_id=1, source_target_pairs={{0,1},{1,0},{2,3},{3,2},{4,5},{5,4},{6,7},{7,6},{8,9},{9,8},{10,11... | collective-permute-start | bytes 2359304 | tf_op jit(solution)/shard_map/ppermute | solution.py:16
  (92 shorter events, 26.9 us)
Async XLA Ops:
  0.6 81.5 %copy-start = (bf16[1,1024,224]{1,2,0:T(8,128)(2,1)S(1)}, bf16[1,1024,224]{1,2,0:T(8,128)(2,1)}, u32[]{:S(2)}) copy-start(bf16[1,1024,224]{1,2,0:T(8,128)(2,1)} %param.14) | copy-start | bytes 1376260
  0.6 4.2 %copy-start.3 = (bf16[16,224]{1,0:T(8,128)(2,1)S(1)}, bf16[16,224]{1,0:T(8,128)(2,1)}, u32[]{:S(2)}) copy-start(bf16[16,224]{1,0:T(8,128)(2,1)} %param.8) | copy-start | bytes 21508
  0.7 4.5 %copy-start.4 = (bf16[16,224]{1,0:T(8,128)(2,1)S(1)}, bf16[16,224]{1,0:T(8,128)(2,1)}, u32[]{:S(2)}) copy-start(bf16[16,224]{1,0:T(8,128)(2,1)} %param.15) | copy-start | bytes 21508
  6.8 74.9 %all-to-all-start = ((bf16[64,4,896]{2,1,0:T(4,128)(2,1)}), bf16[64,4,896]{2,1,0:T(4,128)(2,1)S(1)}, u32[]{:S(2)}, u32[]{:S(2)}) async-start(bf16[64,4,896]{2,1,0:T(4,128)(2,1)} %reshape.181), calls=%async_computation | async-start | bytes 917504 | tf_op jit(solution)/shard_map/all_to_all | solution.py:134
  82.0 1.0 copy-start.2
  82.1 1.2 copy-start.1
  83.6 10.7 %collective-permute-start = (f32[3,128,1024]{2,1,0:T(8,128)S(1)}, f32[3,128,1024]{2,1,0:T(8,128)S(1)}, u32[]{:S(2)}, u32[]{:S(2)}) collective-permute-start(f32[3,128,1024]{2,1,0:T(8,128)S(1)} %pad_maximum_fusion), channel_id=1, source_target_pairs={{0,1},{1,0},{2,3},{3,2},{4,5},{5,4},{6,7},{7,6},{8,9},{9,8},{10,11... | collective-permute-start | bytes 4718600 | tf_op jit(solution)/shard_map/ppermute | solution.py:16
  94.8 9.6 %collective-permute-start.1 = (bf16[3,32,1024]{2,1,0:T(8,128)(2,1)S(1)}, bf16[3,32,1024]{2,1,0:T(8,128)(2,1)S(1)}, u32[]{:S(2)}, u32[]{:S(2)}) collective-permute-start(bf16[3,32,1024]{2,1,0:T(8,128)(2,1)S(1)} %get-tuple-element.15), channel_id=1, source_target_pairs={{0,4},{1,5},{2,6},{3,7},{4,0},{5,1},{6,2},{7,3},{8,12},{9,13},{10,... | collective-permute-start | bytes 589832 | tf_op jit(solution)/shard_map/ppermute | solution.py:16
  97.9 11.3 %collective-permute-start.2 = (bf16[3,32,1024]{2,1,0:T(8,128)(2,1)S(1)}, bf16[3,32,1024]{2,1,0:T(8,128)(2,1)S(1)}, u32[]{:S(2)}, u32[]{:S(2)}) collective-permute-start(bf16[3,32,1024]{2,1,0:T(8,128)(2,1)S(1)} %get-tuple-element.17), channel_id=1, source_target_pairs={{0,8},{1,9},{2,10},{3,11},{4,12},{5,13},{6,14},{7,15},{8,0},{9,1},... | collective-permute-start | bytes 589832 | tf_op jit(solution)/shard_map/ppermute | solution.py:16
  102.3 11.8 %collective-permute-start.3 = (bf16[3,32,1024]{2,1,0:T(8,128)(2,1)S(1)}, bf16[3,32,1024]{2,1,0:T(8,128)(2,1)S(1)}, u32[]{:S(2)}, u32[]{:S(2)}) collective-permute-start(bf16[3,32,1024]{2,1,0:T(8,128)(2,1)S(1)} %get-tuple-element.16), channel_id=1, source_target_pairs={{0,12},{1,13},{2,14},{3,15},{4,8},{5,9},{6,10},{7,11},{8,4},{9,5},... | collective-permute-start | bytes 589832 | tf_op jit(solution)/shard_map/ppermute | solution.py:16
  114.2 50.7 %collective-permute-start.4 = (bf16[3,32,1024]{2,1,0:T(8,128)(2,1)S(1)}, bf16[3,32,1024]{2,1,0:T(8,128)(2,1)S(1)}, u32[]{:S(2)}, u32[]{:S(2)}) collective-permute-start(bf16[3,32,1024]{2,1,0:T(8,128)(2,1)S(1)} %fusion.55), channel_id=1, source_target_pairs={{0,2},{1,3},{2,0},{3,1},{4,6},{5,7},{6,4},{7,5},{8,10},{9,11},{10,... | collective-permute-start | bytes 589832 | tf_op jit(solution)/shard_map/ppermute | solution.py:16
  165.2 9.6 %collective-permute-start.5 = (bf16[3,32,1024]{2,1,0:T(8,128)(2,1)S(1)}, bf16[3,32,1024]{2,1,0:T(8,128)(2,1)S(1)}, u32[]{:S(2)}, u32[]{:S(2)}) collective-permute-start(bf16[3,32,1024]{2,1,0:T(8,128)(2,1)S(1)} %get-tuple-element.24), channel_id=1, source_target_pairs={{0,4},{1,5},{2,6},{3,7},{4,0},{5,1},{6,2},{7,3},{8,12},{9,13},{10,... | collective-permute-start | bytes 589832 | tf_op jit(solution)/shard_map/ppermute | solution.py:16
  167.1 10.3 %collective-permute-start.6 = (bf16[3,32,1024]{2,1,0:T(8,128)(2,1)S(1)}, bf16[3,32,1024]{2,1,0:T(8,128)(2,1)S(1)}, u32[]{:S(2)}, u32[]{:S(2)}) collective-permute-start(bf16[3,32,1024]{2,1,0:T(8,128)(2,1)S(1)} %get-tuple-element.24), channel_id=1, source_target_pairs={{0,8},{1,9},{2,10},{3,11},{4,12},{5,13},{6,14},{7,15},{8,0},{9,1},... | collective-permute-start | bytes 589832 | tf_op jit(solution)/shard_map/ppermute | solution.py:16
  170.4 11.8 %collective-permute-start.7 = (bf16[3,32,1024]{2,1,0:T(8,128)(2,1)S(1)}, bf16[3,32,1024]{2,1,0:T(8,128)(2,1)S(1)}, u32[]{:S(2)}, u32[]{:S(2)}) collective-permute-start(bf16[3,32,1024]{2,1,0:T(8,128)(2,1)S(1)} %get-tuple-element.24), channel_id=1, source_target_pairs={{0,12},{1,13},{2,14},{3,15},{4,8},{5,9},{6,10},{7,11},{8,4},{9,5},... | collective-permute-start | bytes 589832 | tf_op jit(solution)/shard_map/ppermute | solution.py:16
  182.3 4.3 %collective-permute-start.8 = (bf16[3,128,1024]{2,1,0:T(8,128)(2,1)S(1)}, bf16[3,128,1024]{2,1,0:T(8,128)(2,1)S(1)}, u32[]{:S(2)}, u32[]{:S(2)}) collective-permute-start(bf16[3,128,1024]{2,1,0:T(8,128)(2,1)S(1)} %bitcast.122), channel_id=1, source_target_pairs={{0,1},{1,0},{2,3},{3,2},{4,5},{5,4},{6,7},{7,6},{8,9},{9,8},{10,11... | collective-permute-start | bytes 2359304 | tf_op jit(solution)/shard_map/ppermute | solution.py:16
  187.8 29.8 %copy-start.5 = (s32[32]{0:T(128)S(1)}, s32[32]{0:T(128)}, u32[]{:S(2)}) copy-start(s32[32]{0:T(128)} %param.11) | copy-start | bytes 388
  188.8 89.6 %all-to-all-start.1 = ((bf16[64,4,448]{2,1,0:T(4,128)(2,1)}), bf16[64,4,448]{2,1,0:T(4,128)(2,1)S(1)}, u32[]{:S(2)}, u32[]{:S(2)}) async-start(bf16[64,4,448]{2,1,0:T(4,128)(2,1)} %reshape_reshape.7), calls=%async_computation.1 | async-start | bytes 524288 | tf_op jit(solution)/shard_map/all_to_all | solution.py:134
  203.6 32.4 %collective-permute-start.10 = (bf16[3,16,1024]{2,1,0:T(8,128)(2,1)S(1)}, bf16[3,16,1024]{2,1,0:T(8,128)(2,1)S(1)}, u32[]{:S(2)}, u32[]{:S(2)}) collective-permute-start(bf16[3,16,1024]{2,1,0:T(8,128)(2,1)S(1)} %get-tuple-element.21), channel_id=1, source_target_pairs={{0,514},{1,515},{2,512},{3,513},{4,518},{5,519},{6,516},{7,517},{8... | collective-permute-start | bytes 294920 | tf_op jit(solution)/shard_map/ppermute | solution.py:42
  214.8 21.1 %collective-permute-start.9 = (bf16[3,16,1024]{2,1,0:T(8,128)(2,1)S(1)}, bf16[3,16,1024]{2,1,0:T(8,128)(2,1)S(1)}, u32[]{:S(2)}, u32[]{:S(2)}) collective-permute-start(bf16[3,16,1024]{2,1,0:T(8,128)(2,1)S(1)} %get-tuple-element.22), channel_id=1, source_target_pairs={{0,512},{1,513},{2,514},{3,515},{4,516},{5,517},{6,518},{7,519},{8... | collective-permute-start | bytes 294920 | tf_op jit(solution)/shard_map/ppermute | solution.py:42
  236.0 9.7 %collective-permute-start.11 = (bf16[3,32,1024]{2,1,0:T(8,128)(2,1)S(1)}, bf16[3,32,1024]{2,1,0:T(8,128)(2,1)S(1)}, u32[]{:S(2)}, u32[]{:S(2)}) collective-permute-start(bf16[3,32,1024]{2,1,0:T(8,128)(2,1)S(1)} %maximum_select_fusion.1), channel_id=1, source_target_pairs={{0,4},{1,5},{2,6},{3,7},{4,0},{5,1},{6,2},{7,3},{8,12},{9,13},{10,... | collective-permute-start | bytes 589832 | tf_op jit(solution)/shard_map/ppermute | solution.py:16
  238.7 8.3 %collective-permute-start.12 = (bf16[3,32,1024]{2,1,0:T(8,128)(2,1)S(1)}, bf16[3,32,1024]{2,1,0:T(8,128)(2,1)S(1)}, u32[]{:S(2)}, u32[]{:S(2)}) collective-permute-start(bf16[3,32,1024]{2,1,0:T(8,128)(2,1)S(1)} %maximum_select_fusion.1), channel_id=1, source_target_pairs={{0,8},{1,9},{2,10},{3,11},{4,12},{5,13},{6,14},{7,15},{8,0},{9,1},... | collective-permute-start | bytes 589832 | tf_op jit(solution)/shard_map/ppermute | solution.py:16
  243.5 7.9 %collective-permute-start.13 = (bf16[3,32,1024]{2,1,0:T(8,128)(2,1)S(1)}, bf16[3,32,1024]{2,1,0:T(8,128)(2,1)S(1)}, u32[]{:S(2)}, u32[]{:S(2)}) collective-permute-start(bf16[3,32,1024]{2,1,0:T(8,128)(2,1)S(1)} %maximum_select_fusion.1), channel_id=1, source_target_pairs={{0,12},{1,13},{2,14},{3,15},{4,8},{5,9},{6,10},{7,11},{8,4},{9,5},... | collective-permute-start | bytes 589832 | tf_op jit(solution)/shard_map/ppermute | solution.py:16
  251.6 23.3 %collective-permute-start.14 = (bf16[3,128,1024]{2,1,0:T(8,128)(2,1)S(1)}, bf16[3,128,1024]{2,1,0:T(8,128)(2,1)S(1)}, u32[]{:S(2)}, u32[]{:S(2)}) collective-permute-start(bf16[3,128,1024]{2,1,0:T(8,128)(2,1)S(1)} %bitcast.126), channel_id=1, source_target_pairs={{0,1},{1,0},{2,3},{3,2},{4,5},{5,4},{6,7},{7,6},{8,9},{9,8},{10,11... | collective-permute-start | bytes 2359304 | tf_op jit(solution)/shard_map/ppermute | solution.py:16

commit v2 on v0

--- a/solution.py
+++ b/solution.py
@@ -152,7 +152,9 @@
         )
 
     other_rows = core_swap(partial_sums(rows[half_rows:]))
-    their_rows = partner(rows)
+    in_rows, grad_in = rows[:, :feat_width], rows[:, feat_width:]
+    their_in = partner(in_rows)
+    their_grad = partner(grad_in)
     sums = partial_sums(rows[:half_rows]) + other_rows
     sums = reduce_over_x(sums.reshape(3, X_CHIPS, slot_total // PARTS, hidden_width))
     sums = sums + z_swap(sums.astype(BF16)).astype(F32)
@@ -179,8 +181,8 @@
     returned = trade(relative_blocks(back, core, x))
 
     hidden, gate_grad, up_grad = gather_all(held_factors)
-    held_rows = jnp.where(my_flag == 1, their_rows, rows)
-    in_rows, grad_in = held_rows[:, :feat_width], held_rows[:, feat_width:]
+    in_rows = jnp.where(my_flag == 1, their_in, in_rows)
+    grad_in = jnp.where(my_flag == 1, their_grad, grad_in)
     grads = (
         contract_first(gate_grad, in_rows).astype(BF16),
         contract_first(up_grad, in_rows).astype(BF16),

time: 306 us -> 281 us (0.918)
  the two profiles are of different devices: /device:TPU:33 before, /device:TPU:6 now
where the time goes in v2:
time: 281 us; the launch traced here: 277 us
  waiting for transfers between devices  141 us (50%)
  starting transfers between devices  118 us (42%)
  matrix products  8.74 us (3%)
  local copies, waits for them, and re-layouts  3.98 us (1%)
    ppermute x13, waiting for transfers between devices, exchanged(): return lax.ppermute(value, 'dp', [(i, i ^ mask) for i in range(size)])  63.8 us
    ppermute x13, starting transfers between devices, exchanged(): return lax.ppermute(value, 'dp', [(i, i ^ mask) for i in range(size)])  48.9 us
    ppermute x2, waiting for transfers between devices, partner(): lax.ppermute(value, 'expert', [(i, (i + experts // 2) % experts) for i in...  42.9 us
    all_to_all x2, starting transfers between devices, trade(): lax.all_to_all(outbound.reshape(experts, capacity, outbound.shape[1]), 'e...  40.3 us
    all_to_all x2, waiting for transfers between devices, trade(): lax.all_to_all(outbound.reshape(experts, capacity, outbound.shape[1]), 'e...  34.5 us
    ppermute x2, starting transfers between devices, partner(): lax.ppermute(value, 'expert', [(i, (i + experts // 2) % experts) for i in...  14.6 us
    ppermute x2, starting transfers between devices, along_z(): return lax.ppermute(value, ('expert', 'dp'), pairs)  14.6 us
  transfers between devices with their start and end apart: 19, of which 11 were waited for; matrix products, arithmetic and copies ran while one was open for 3% of the time, Pallas kernels for 0%

profile of v2, /device:TPU:6, one launch (start us, length us, event | category | flops | bytes accessed | tf_op | source)
XLA Modules:
  0.0 277.0 jit_solution(1300308335659616984)
XLA Ops:
  4.6 29.4 %all-to-all-start = ((bf16[64,4,448]{2,1,0:T(4,128)(2,1)}), bf16[64,4,448]{2,1,0:T(4,128)(2,1)S(1)}, u32[]{:S(2)}, u32[]{:S(2)}) async-start(bf16[64,4,448]{2,1,0:T(4,128)(2,1)} %reshape.135), calls=%async_computation | async-start | bytes 524288 | tf_op jit(solution)/shard_map/all_to_all | solution.py:127
  34.1 34.5 %all-to-all-done = bf16[64,4,448]{2,1,0:T(4,128)(2,1)S(1)} async-done(((bf16[64,4,448]{2,1,0:T(4,128)(2,1)}), bf16[64,4,448]{2,1,0:T(4,128)(2,1)S(1)}, u32[]{:S(2)}, u32[]{:S(2)}) %all-to-all-start) | async-done | bytes 229408 | tf_op jit(solution)/shard_map/all_to_all | solution.py:127
  73.1 2.6 collective-permute-done
  76.2 2.7 collective-permute-start.1
  78.9 3.0 %collective-permute-start.2 = (bf16[3,32,1024]{2,1,0:T(8,128)(2,1)S(1)}, bf16[3,32,1024]{2,1,0:T(8,128)(2,1)S(1)}, u32[]{:S(2)}, u32[]{:S(2)}) collective-permute-start(bf16[3,32,1024]{2,1,0:T(8,128)(2,1)S(1)} %get-tuple-element.13), channel_id=1, source_target_pairs={{0,8},{1,9},{2,10},{3,11},{4,12},{5,13},{6,14},{7,15},{8,0},{9,1},... | collective-permute-start | bytes 589832 | tf_op jit(solution)/shard_map/ppermute | solution.py:16
  81.9 4.7 %collective-permute-start.3 = (bf16[3,32,1024]{2,1,0:T(8,128)(2,1)S(1)}, bf16[3,32,1024]{2,1,0:T(8,128)(2,1)S(1)}, u32[]{:S(2)}, u32[]{:S(2)}) collective-permute-start(bf16[3,32,1024]{2,1,0:T(8,128)(2,1)S(1)} %get-tuple-element.12), channel_id=1, source_target_pairs={{0,12},{1,13},{2,14},{3,15},{4,8},{5,9},{6,10},{7,11},{8,4},{9,5},... | collective-permute-start | bytes 589832 | tf_op jit(solution)/shard_map/ppermute | solution.py:16
  86.6 2.6 collective-permute-done.2
  89.2 4.1 %collective-permute-done.3 = bf16[3,32,1024]{2,1,0:T(8,128)(2,1)S(1)} collective-permute-done((bf16[3,32,1024]{2,1,0:T(8,128)(2,1)S(1)}, bf16[3,32,1024]{2,1,0:T(8,128)(2,1)S(1)}, u32[]{:S(2)}, u32[]{:S(2)}) %collective-permute-start.3) | collective-permute-done | bytes 196640 | tf_op jit(solution)/shard_map/ppermute | solution.py:16
  93.5 11.9 %collective-permute-start.4 = (bf16[3,32,1024]{2,1,0:T(8,128)(2,1)S(1)}, bf16[3,32,1024]{2,1,0:T(8,128)(2,1)S(1)}, u32[]{:S(2)}, u32[]{:S(2)}) collective-permute-start(bf16[3,32,1024]{2,1,0:T(8,128)(2,1)S(1)} %fusion.54), channel_id=1, source_target_pairs={{0,2},{1,3},{2,0},{3,1},{4,6},{5,7},{6,4},{7,5},{8,10},{9,11},{10,... | collective-permute-start | bytes 589832 | tf_op jit(solution)/shard_map/ppermute | solution.py:16
  105.3 39.5 %collective-permute-done.4 = bf16[3,32,1024]{2,1,0:T(8,128)(2,1)S(1)} collective-permute-done((bf16[3,32,1024]{2,1,0:T(8,128)(2,1)S(1)}, bf16[3,32,1024]{2,1,0:T(8,128)(2,1)S(1)}, u32[]{:S(2)}, u32[]{:S(2)}) %collective-permute-start.4) | collective-permute-done | bytes 196640 | tf_op jit(solution)/shard_map/ppermute | solution.py:16
  145.1 2.9 %collective-permute-start.5 = (bf16[3,32,1024]{2,1,0:T(8,128)(2,1)S(1)}, bf16[3,32,1024]{2,1,0:T(8,128)(2,1)S(1)}, u32[]{:S(2)}, u32[]{:S(2)}) collective-permute-start(bf16[3,32,1024]{2,1,0:T(8,128)(2,1)S(1)} %get-tuple-element.24), channel_id=1, source_target_pairs={{0,4},{1,5},{2,6},{3,7},{4,0},{5,1},{6,2},{7,3},{8,12},{9,13},{10,... | collective-permute-start | bytes 589832 | tf_op jit(solution)/shard_map/ppermute | solution.py:16
  148.0 5.1 %collective-permute-start.6 = (bf16[3,32,1024]{2,1,0:T(8,128)(2,1)S(1)}, bf16[3,32,1024]{2,1,0:T(8,128)(2,1)S(1)}, u32[]{:S(2)}, u32[]{:S(2)}) collective-permute-start(bf16[3,32,1024]{2,1,0:T(8,128)(2,1)S(1)} %get-tuple-element.24), channel_id=1, source_target_pairs={{0,8},{1,9},{2,10},{3,11},{4,12},{5,13},{6,14},{7,15},{8,0},{9,1},... | collective-permute-start | bytes 589832 | tf_op jit(solution)/shard_map/ppermute | solution.py:16
  153.1 2.4 collective-permute-start.7
  155.5 4.7 %collective-permute-done.6 = bf16[3,32,1024]{2,1,0:T(8,128)(2,1)S(1)} collective-permute-done((bf16[3,32,1024]{2,1,0:T(8,128)(2,1)S(1)}, bf16[3,32,1024]{2,1,0:T(8,128)(2,1)S(1)}, u32[]{:S(2)}, u32[]{:S(2)}) %collective-permute-start.6) | collective-permute-done | bytes 196640 | tf_op jit(solution)/shard_map/ppermute | solution.py:16
  160.2 4.1 %collective-permute-done.7 = bf16[3,32,1024]{2,1,0:T(8,128)(2,1)S(1)} collective-permute-done((bf16[3,32,1024]{2,1,0:T(8,128)(2,1)S(1)}, bf16[3,32,1024]{2,1,0:T(8,128)(2,1)S(1)}, u32[]{:S(2)}, u32[]{:S(2)}) %collective-permute-start.7) | collective-permute-done | bytes 196640 | tf_op jit(solution)/shard_map/ppermute | solution.py:16
  168.3 12.6 %collective-permute-start.9 = (bf16[3,16,1024]{2,1,0:T(8,128)(2,1)S(1)}, bf16[3,16,1024]{2,1,0:T(8,128)(2,1)S(1)}, u32[]{:S(2)}, u32[]{:S(2)}) collective-permute-start(bf16[3,16,1024]{2,1,0:T(8,128)(2,1)S(1)} %get-tuple-element.22), channel_id=1, source_target_pairs={{0,512},{1,513},{2,514},{3,515},{4,516},{5,517},{6,518},{7,519},{8... | collective-permute-start | bytes 294920 | tf_op jit(solution)/shard_map/ppermute | solution.py:42
  183.1 10.9 %all-to-all-start.1 = ((bf16[64,4,448]{2,1,0:T(4,128)(2,1)}), bf16[64,4,448]{2,1,0:T(4,128)(2,1)S(1)}, u32[]{:S(2)}, u32[]{:S(2)}) async-start(bf16[64,4,448]{2,1,0:T(4,128)(2,1)} %reshape_reshape.7), calls=%async_computation.1 | async-start | bytes 524288 | tf_op jit(solution)/shard_map/all_to_all | solution.py:127
  197.3 3.8 %collective-permute-start.12 = (bf16[3,32,1024]{2,1,0:T(8,128)(2,1)S(1)}, bf16[3,32,1024]{2,1,0:T(8,128)(2,1)S(1)}, u32[]{:S(2)}, u32[]{:S(2)}) collective-permute-start(bf16[3,32,1024]{2,1,0:T(8,128)(2,1)S(1)} %maximum_select_fusion.1), channel_id=1, source_target_pairs={{0,8},{1,9},{2,10},{3,11},{4,12},{5,13},{6,14},{7,15},{8,0},{9,1},... | collective-permute-start | bytes 589832 | tf_op jit(solution)/shard_map/ppermute | solution.py:16
  201.1 4.7 %collective-permute-start.13 = (bf16[3,32,1024]{2,1,0:T(8,128)(2,1)S(1)}, bf16[3,32,1024]{2,1,0:T(8,128)(2,1)S(1)}, u32[]{:S(2)}, u32[]{:S(2)}) collective-permute-start(bf16[3,32,1024]{2,1,0:T(8,128)(2,1)S(1)} %maximum_select_fusion.1), channel_id=1, source_target_pairs={{0,12},{1,13},{2,14},{3,15},{4,8},{5,9},{6,10},{7,11},{8,4},{9,5},... | collective-permute-start | bytes 589832 | tf_op jit(solution)/shard_map/ppermute | solution.py:16
  205.9 2.1 collective-permute-done.12
  208.0 4.1 %collective-permute-done.13 = bf16[3,32,1024]{2,1,0:T(8,128)(2,1)S(1)} collective-permute-done((bf16[3,32,1024]{2,1,0:T(8,128)(2,1)S(1)}, bf16[3,32,1024]{2,1,0:T(8,128)(2,1)S(1)}, u32[]{:S(2)}, u32[]{:S(2)}) %collective-permute-start.13) | collective-permute-done | bytes 196640 | tf_op jit(solution)/shard_map/ppermute | solution.py:16
  214.3 12.0 %collective-permute-start.16 = (bf16[256,224]{1,0:T(8,128)(2,1)S(1)}, bf16[256,224]{1,0:T(8,128)(2,1)S(1)}, u32[]{:S(2)}, u32[]{:S(2)}) collective-permute-start(bf16[256,224]{1,0:T(8,128)(2,1)S(1)} %get-tuple-element.17), channel_id=1, source_target_pairs={{0,512},{16,528},{32,544},{48,560},{64,576},{80,592},{96,608},{112... | collective-permute-start | bytes 344072 | tf_op jit(solution)/shard_map/ppermute | solution.py:47
  226.3 2.5 collective-permute-start.15
  228.9 41.7 %collective-permute-done.16 = bf16[256,224]{1,0:T(8,128)(2,1)S(1)} collective-permute-done((bf16[256,224]{1,0:T(8,128)(2,1)S(1)}, bf16[256,224]{1,0:T(8,128)(2,1)S(1)}, u32[]{:S(2)}, u32[]{:S(2)}) %collective-permute-start.16) | collective-permute-done | bytes 114720 | tf_op jit(solution)/shard_map/ppermute | solution.py:47
  (83 shorter events, 26.2 us)
Async XLA Ops:
  0.6 68.3 %copy-start = (bf16[1,1024,224]{1,2,0:T(8,128)(2,1)S(1)}, bf16[1,1024,224]{1,2,0:T(8,128)(2,1)}, u32[]{:S(2)}) copy-start(bf16[1,1024,224]{1,2,0:T(8,128)(2,1)} %param.14) | copy-start | bytes 1376260
  4.6 64.0 %all-to-all-start = ((bf16[64,4,448]{2,1,0:T(4,128)(2,1)}), bf16[64,4,448]{2,1,0:T(4,128)(2,1)S(1)}, u32[]{:S(2)}, u32[]{:S(2)}) async-start(bf16[64,4,448]{2,1,0:T(4,128)(2,1)} %reshape.135), calls=%async_computation | async-start | bytes 524288 | tf_op jit(solution)/shard_map/all_to_all | solution.py:127
  68.7 1.0 copy-start.2
  68.9 1.1 copy-start.1
  70.4 5.3 %collective-permute-start = (f32[3,128,1024]{2,1,0:T(8,128)S(1)}, f32[3,128,1024]{2,1,0:T(8,128)S(1)}, u32[]{:S(2)}, u32[]{:S(2)}) collective-permute-start(f32[3,128,1024]{2,1,0:T(8,128)S(1)} %pad_maximum_fusion), channel_id=1, source_target_pairs={{0,1},{1,0},{2,3},{3,2},{4,5},{5,4},{6,7},{7,6},{8,9},{9,8},{10,11... | collective-permute-start | bytes 4718600 | tf_op jit(solution)/shard_map/ppermute | solution.py:16
  76.2 10.5 %collective-permute-start.1 = (bf16[3,32,1024]{2,1,0:T(8,128)(2,1)S(1)}, bf16[3,32,1024]{2,1,0:T(8,128)(2,1)S(1)}, u32[]{:S(2)}, u32[]{:S(2)}) collective-permute-start(bf16[3,32,1024]{2,1,0:T(8,128)(2,1)S(1)} %get-tuple-element.11), channel_id=1, source_target_pairs={{0,4},{1,5},{2,6},{3,7},{4,0},{5,1},{6,2},{7,3},{8,12},{9,13},{10,... | collective-permute-start | bytes 589832 | tf_op jit(solution)/shard_map/ppermute | solution.py:16
  78.9 10.3 %collective-permute-start.2 = (bf16[3,32,1024]{2,1,0:T(8,128)(2,1)S(1)}, bf16[3,32,1024]{2,1,0:T(8,128)(2,1)S(1)}, u32[]{:S(2)}, u32[]{:S(2)}) collective-permute-start(bf16[3,32,1024]{2,1,0:T(8,128)(2,1)S(1)} %get-tuple-element.13), channel_id=1, source_target_pairs={{0,8},{1,9},{2,10},{3,11},{4,12},{5,13},{6,14},{7,15},{8,0},{9,1},... | collective-permute-start | bytes 589832 | tf_op jit(solution)/shard_map/ppermute | solution.py:16
  81.9 11.4 %collective-permute-start.3 = (bf16[3,32,1024]{2,1,0:T(8,128)(2,1)S(1)}, bf16[3,32,1024]{2,1,0:T(8,128)(2,1)S(1)}, u32[]{:S(2)}, u32[]{:S(2)}) collective-permute-start(bf16[3,32,1024]{2,1,0:T(8,128)(2,1)S(1)} %get-tuple-element.12), channel_id=1, source_target_pairs={{0,12},{1,13},{2,14},{3,15},{4,8},{5,9},{6,10},{7,11},{8,4},{9,5},... | collective-permute-start | bytes 589832 | tf_op jit(solution)/shard_map/ppermute | solution.py:16
  93.5 51.4 %collective-permute-start.4 = (bf16[3,32,1024]{2,1,0:T(8,128)(2,1)S(1)}, bf16[3,32,1024]{2,1,0:T(8,128)(2,1)S(1)}, u32[]{:S(2)}, u32[]{:S(2)}) collective-permute-start(bf16[3,32,1024]{2,1,0:T(8,128)(2,1)S(1)} %fusion.54), channel_id=1, source_target_pairs={{0,2},{1,3},{2,0},{3,1},{4,6},{5,7},{6,4},{7,5},{8,10},{9,11},{10,... | collective-permute-start | bytes 589832 | tf_op jit(solution)/shard_map/ppermute | solution.py:16
  145.1 10.5 %collective-permute-start.5 = (bf16[3,32,1024]{2,1,0:T(8,128)(2,1)S(1)}, bf16[3,32,1024]{2,1,0:T(8,128)(2,1)S(1)}, u32[]{:S(2)}, u32[]{:S(2)}) collective-permute-start(bf16[3,32,1024]{2,1,0:T(8,128)(2,1)S(1)} %get-tuple-element.24), channel_id=1, source_target_pairs={{0,4},{1,5},{2,6},{3,7},{4,0},{5,1},{6,2},{7,3},{8,12},{9,13},{10,... | collective-permute-start | bytes 589832 | tf_op jit(solution)/shard_map/ppermute | solution.py:16
  148.0 12.2 %collective-permute-start.6 = (bf16[3,32,1024]{2,1,0:T(8,128)(2,1)S(1)}, bf16[3,32,1024]{2,1,0:T(8,128)(2,1)S(1)}, u32[]{:S(2)}, u32[]{:S(2)}) collective-permute-start(bf16[3,32,1024]{2,1,0:T(8,128)(2,1)S(1)} %get-tuple-element.24), channel_id=1, source_target_pairs={{0,8},{1,9},{2,10},{3,11},{4,12},{5,13},{6,14},{7,15},{8,0},{9,1},... | collective-permute-start | bytes 589832 | tf_op jit(solution)/shard_map/ppermute | solution.py:16
  153.1 11.2 %collective-permute-start.7 = (bf16[3,32,1024]{2,1,0:T(8,128)(2,1)S(1)}, bf16[3,32,1024]{2,1,0:T(8,128)(2,1)S(1)}, u32[]{:S(2)}, u32[]{:S(2)}) collective-permute-start(bf16[3,32,1024]{2,1,0:T(8,128)(2,1)S(1)} %get-tuple-element.24), channel_id=1, source_target_pairs={{0,12},{1,13},{2,14},{3,15},{4,8},{5,9},{6,10},{7,11},{8,4},{9,5},... | collective-permute-start | bytes 589832 | tf_op jit(solution)/shard_map/ppermute | solution.py:16
  164.4 16.5 %collective-permute-start.8 = (bf16[3,128,1024]{2,1,0:T(8,128)(2,1)S(1)}, bf16[3,128,1024]{2,1,0:T(8,128)(2,1)S(1)}, u32[]{:S(2)}, u32[]{:S(2)}) collective-permute-start(bf16[3,128,1024]{2,1,0:T(8,128)(2,1)S(1)} %bitcast.119), channel_id=1, source_target_pairs={{0,1},{1,0},{2,3},{3,2},{4,5},{5,4},{6,7},{7,6},{8,9},{9,8},{10,11... | collective-permute-start | bytes 2359304 | tf_op jit(solution)/shard_map/ppermute | solution.py:16
  166.4 28.9 %collective-permute-start.10 = (bf16[3,16,1024]{2,1,0:T(8,128)(2,1)S(1)}, bf16[3,16,1024]{2,1,0:T(8,128)(2,1)S(1)}, u32[]{:S(2)}, u32[]{:S(2)}) collective-permute-start(bf16[3,16,1024]{2,1,0:T(8,128)(2,1)S(1)} %get-tuple-element.21), channel_id=1, source_target_pairs={{0,514},{1,515},{2,512},{3,513},{4,518},{5,519},{6,516},{7,517},{8... | collective-permute-start | bytes 294920 | tf_op jit(solution)/shard_map/ppermute | solution.py:42
  168.3 27.0 %collective-permute-start.9 = (bf16[3,16,1024]{2,1,0:T(8,128)(2,1)S(1)}, bf16[3,16,1024]{2,1,0:T(8,128)(2,1)S(1)}, u32[]{:S(2)}, u32[]{:S(2)}) collective-permute-start(bf16[3,16,1024]{2,1,0:T(8,128)(2,1)S(1)} %get-tuple-element.22), channel_id=1, source_target_pairs={{0,512},{1,513},{2,514},{3,515},{4,516},{5,517},{6,518},{7,519},{8... | collective-permute-start | bytes 294920 | tf_op jit(solution)/shard_map/ppermute | solution.py:42
  182.1 12.0 %copy-start.3 = (s32[32]{0:T(128)S(1)}, s32[32]{0:T(128)}, u32[]{:S(2)}) copy-start(s32[32]{0:T(128)} %param.11) | copy-start | bytes 388
  183.1 92.0 %all-to-all-start.1 = ((bf16[64,4,448]{2,1,0:T(4,128)(2,1)}), bf16[64,4,448]{2,1,0:T(4,128)(2,1)S(1)}, u32[]{:S(2)}, u32[]{:S(2)}) async-start(bf16[64,4,448]{2,1,0:T(4,128)(2,1)} %reshape_reshape.7), calls=%async_computation.1 | async-start | bytes 524288 | tf_op jit(solution)/shard_map/all_to_all | solution.py:127
  195.4 10.5 %collective-permute-start.11 = (bf16[3,32,1024]{2,1,0:T(8,128)(2,1)S(1)}, bf16[3,32,1024]{2,1,0:T(8,128)(2,1)S(1)}, u32[]{:S(2)}, u32[]{:S(2)}) collective-permute-start(bf16[3,32,1024]{2,1,0:T(8,128)(2,1)S(1)} %maximum_select_fusion.1), channel_id=1, source_target_pairs={{0,4},{1,5},{2,6},{3,7},{4,0},{5,1},{6,2},{7,3},{8,12},{9,13},{10,... | collective-permute-start | bytes 589832 | tf_op jit(solution)/shard_map/ppermute | solution.py:16
  197.3 10.7 %collective-permute-start.12 = (bf16[3,32,1024]{2,1,0:T(8,128)(2,1)S(1)}, bf16[3,32,1024]{2,1,0:T(8,128)(2,1)S(1)}, u32[]{:S(2)}, u32[]{:S(2)}) collective-permute-start(bf16[3,32,1024]{2,1,0:T(8,128)(2,1)S(1)} %maximum_select_fusion.1), channel_id=1, source_target_pairs={{0,8},{1,9},{2,10},{3,11},{4,12},{5,13},{6,14},{7,15},{8,0},{9,1},... | collective-permute-start | bytes 589832 | tf_op jit(solution)/shard_map/ppermute | solution.py:16
  201.1 10.9 %collective-permute-start.13 = (bf16[3,32,1024]{2,1,0:T(8,128)(2,1)S(1)}, bf16[3,32,1024]{2,1,0:T(8,128)(2,1)S(1)}, u32[]{:S(2)}, u32[]{:S(2)}) collective-permute-start(bf16[3,32,1024]{2,1,0:T(8,128)(2,1)S(1)} %maximum_select_fusion.1), channel_id=1, source_target_pairs={{0,12},{1,13},{2,14},{3,15},{4,8},{5,9},{6,10},{7,11},{8,4},{9,5},... | collective-permute-start | bytes 589832 | tf_op jit(solution)/shard_map/ppermute | solution.py:16
  212.2 58.3 %collective-permute-start.14 = (bf16[3,128,1024]{2,1,0:T(8,128)(2,1)S(1)}, bf16[3,128,1024]{2,1,0:T(8,128)(2,1)S(1)}, u32[]{:S(2)}, u32[]{:S(2)}) collective-permute-start(bf16[3,128,1024]{2,1,0:T(8,128)(2,1)S(1)} %bitcast.115), channel_id=1, source_target_pairs={{0,1},{1,0},{2,3},{3,2},{4,5},{5,4},{6,7},{7,6},{8,9},{9,8},{10,11... | collective-permute-start | bytes 2359304 | tf_op jit(solution)/shard_map/ppermute | solution.py:16
  214.3 56.3 %collective-permute-start.16 = (bf16[256,224]{1,0:T(8,128)(2,1)S(1)}, bf16[256,224]{1,0:T(8,128)(2,1)S(1)}, u32[]{:S(2)}, u32[]{:S(2)}) collective-permute-start(bf16[256,224]{1,0:T(8,128)(2,1)S(1)} %get-tuple-element.17), channel_id=1, source_target_pairs={{0,512},{16,528},{32,544},{48,560},{64,576},{80,592},{96,608},{112... | collective-permute-start | bytes 344072 | tf_op jit(solution)/shard_map/ppermute | solution.py:47
  226.3 46.6 %collective-permute-start.15 = (bf16[256,224]{1,0:T(8,128)(2,1)S(1)}, bf16[256,224]{1,0:T(8,128)(2,1)S(1)}, u32[]{:S(2)}, u32[]{:S(2)}) collective-permute-start(bf16[256,224]{1,0:T(8,128)(2,1)S(1)} %get-tuple-element.18), channel_id=1, source_target_pairs={{0,512},{16,528},{32,544},{48,560},{64,576},{80,592},{96,608},{112... | collective-permute-start | bytes 344072 | tf_op jit(solution)/shard_map/ppermute | solution.py:47

commit v3 on v1

--- a/solution.py
+++ b/solution.py
@@ -28,7 +28,7 @@
     return exchanged(value, mask * CORES * Z_HALVES)
 
 
-def along_z(value, shift):
+def to_partner(value):
     experts, shards = lax.axis_size("expert"), lax.axis_size("dp")
     low = experts // Y_CHIPS
     pairs = []
@@ -36,6 +36,7 @@
         place, y = divmod(expert, Y_CHIPS)
         for d in range(shards):
             x, half, core = d // 4, (d // 2) % 2, d % 2
+            shift = -(low // 2) if core else low // 2
             z = (half * low + place + shift) % (Z_HALVES * low)
             goal = (z % low) * Y_CHIPS + y
             pairs.append((expert * shards + d, goal * shards + x * 4 + (z // low) * 2 + core))
@@ -164,16 +165,12 @@
             (hidden_grad * activated).astype(BF16),
         ]
     )
-    cut = factors.shape[1] // 2
-    reach = experts // Y_CHIPS // 2
-    first_cut = along_z(factors[:, :cut], reach)
-    second_cut = along_z(factors[:, cut:], -reach)
+    theirs = to_partner(factors)
     hidden, gate_grad, up_grad = gather_all(factors)
     expert_out = contract_last(hidden, down_w).astype(BF16)
     row_back = (contract_last(gate_grad, gate_w) + contract_last(up_grad, up_w)).astype(BF16)
     back = jnp.concatenate([expert_out, row_back], axis=1)
-    first_cut, second_cut, _ = lax.optimization_barrier((first_cut, second_cut, back))
-    theirs = jnp.concatenate([first_cut, second_cut], axis=1)
+    theirs, _ = lax.optimization_barrier((theirs, back))
     held_factors = jnp.where(my_flag == 1, theirs, factors)
     returned = trade(relative_blocks(back, core, x))
 

time: 281 us -> 261 us (0.929)
  the two profiles are of different devices: /device:TPU:33 before, /device:TPU:6 now
where the time goes in v3:
time: 261 us; the launch traced here: 260 us
  waiting for transfers between devices  139 us (53%)
  starting transfers between devices  99.8 us (38%)
  matrix products  9.62 us (4%)
  other arithmetic  5.4 us (2%)
  local copies, waits for them, and re-layouts  4.71 us (2%)
    ppermute x13, waiting for transfers between devices, exchanged(): return lax.ppermute(value, 'dp', [(i, i ^ mask) for i in range(size)])  67.2 us
    all_to_all x2, waiting for transfers between devices, trade(): lax.all_to_all(outbound.reshape(experts, capacity, outbound.shape[1]), 'e...  58 us
    all_to_all x2, starting transfers between devices, trade(): lax.all_to_all(outbound.reshape(experts, capacity, outbound.shape[1]), 'e...  49 us
    ppermute x13, starting transfers between devices, exchanged(): return lax.ppermute(value, 'dp', [(i, i ^ mask) for i in range(size)])  48.9 us
    ppermute x1, waiting for transfers between devices, to_partner(): return lax.ppermute(value, ('expert', 'dp'), pairs)  13.6 us
  transfers between devices with their start and end apart: 16, of which 12 were waited for; matrix products, arithmetic and copies ran while one was open for 3% of the time, Pallas kernels for 0%

profile of v3, /device:TPU:6, one launch (start us, length us, event | category | flops | bytes accessed | tf_op | source)
XLA Modules:
  0.0 260.3 jit_solution(605154633974434968)
XLA Ops:
  6.9 29.4 %all-to-all-start = ((bf16[64,4,896]{2,1,0:T(4,128)(2,1)}), bf16[64,4,896]{2,1,0:T(4,128)(2,1)S(1)}, u32[]{:S(2)}, u32[]{:S(2)}) async-start(bf16[64,4,896]{2,1,0:T(4,128)(2,1)} %reshape.113), calls=%async_computation | async-start | bytes 917504 | tf_op jit(solution)/shard_map/all_to_all | solution.py:135
  36.3 48.8 %all-to-all-done = bf16[64,4,896]{2,1,0:T(4,128)(2,1)S(1)} async-done(((bf16[64,4,896]{2,1,0:T(4,128)(2,1)}), bf16[64,4,896]{2,1,0:T(4,128)(2,1)S(1)}, u32[]{:S(2)}, u32[]{:S(2)}) %all-to-all-start) | async-done | bytes 458784 | tf_op jit(solution)/shard_map/all_to_all | solution.py:135
  89.9 2.6 %collective-permute-done = f32[3,128,1024]{2,1,0:T(8,128)S(1)} collective-permute-done((f32[3,128,1024]{2,1,0:T(8,128)S(1)}, f32[3,128,1024]{2,1,0:T(8,128)S(1)}, u32[]{:S(2)}, u32[]{:S(2)}) %collective-permute-start) | collective-permute-done | bytes 1572896 | tf_op jit(solution)/shard_map/ppermute | solution.py:16
  93.0 2.7 %collective-permute-start.1 = (bf16[3,32,1024]{2,1,0:T(8,128)(2,1)S(1)}, bf16[3,32,1024]{2,1,0:T(8,128)(2,1)S(1)}, u32[]{:S(2)}, u32[]{:S(2)}) collective-permute-start(bf16[3,32,1024]{2,1,0:T(8,128)(2,1)S(1)} %get-tuple-element.13), channel_id=1, source_target_pairs={{0,4},{1,5},{2,6},{3,7},{4,0},{5,1},{6,2},{7,3},{8,12},{9,13},{10,... | collective-permute-start | bytes 589832 | tf_op jit(solution)/shard_map/ppermute | solution.py:16
  95.7 3.0 %collective-permute-start.2 = (bf16[3,32,1024]{2,1,0:T(8,128)(2,1)S(1)}, bf16[3,32,1024]{2,1,0:T(8,128)(2,1)S(1)}, u32[]{:S(2)}, u32[]{:S(2)}) collective-permute-start(bf16[3,32,1024]{2,1,0:T(8,128)(2,1)S(1)} %get-tuple-element.15), channel_id=1, source_target_pairs={{0,8},{1,9},{2,10},{3,11},{4,12},{5,13},{6,14},{7,15},{8,0},{9,1},... | collective-permute-start | bytes 589832 | tf_op jit(solution)/shard_map/ppermute | solution.py:16
  98.8 4.7 %collective-permute-start.3 = (bf16[3,32,1024]{2,1,0:T(8,128)(2,1)S(1)}, bf16[3,32,1024]{2,1,0:T(8,128)(2,1)S(1)}, u32[]{:S(2)}, u32[]{:S(2)}) collective-permute-start(bf16[3,32,1024]{2,1,0:T(8,128)(2,1)S(1)} %get-tuple-element.14), channel_id=1, source_target_pairs={{0,12},{1,13},{2,14},{3,15},{4,8},{5,9},{6,10},{7,11},{8,4},{9,5},... | collective-permute-start | bytes 589832 | tf_op jit(solution)/shard_map/ppermute | solution.py:16
  103.4 2.6 %collective-permute-done.2 = bf16[3,32,1024]{2,1,0:T(8,128)(2,1)S(1)} collective-permute-done((bf16[3,32,1024]{2,1,0:T(8,128)(2,1)S(1)}, bf16[3,32,1024]{2,1,0:T(8,128)(2,1)S(1)}, u32[]{:S(2)}, u32[]{:S(2)}) %collective-permute-start.2) | collective-permute-done | bytes 196640 | tf_op jit(solution)/shard_map/ppermute | solution.py:16
  106.0 4.1 %collective-permute-done.3 = bf16[3,32,1024]{2,1,0:T(8,128)(2,1)S(1)} collective-permute-done((bf16[3,32,1024]{2,1,0:T(8,128)(2,1)S(1)}, bf16[3,32,1024]{2,1,0:T(8,128)(2,1)S(1)}, u32[]{:S(2)}, u32[]{:S(2)}) %collective-permute-start.3) | collective-permute-done | bytes 196640 | tf_op jit(solution)/shard_map/ppermute | solution.py:16
  110.3 11.9 %collective-permute-start.4 = (bf16[3,32,1024]{2,1,0:T(8,128)(2,1)S(1)}, bf16[3,32,1024]{2,1,0:T(8,128)(2,1)S(1)}, u32[]{:S(2)}, u32[]{:S(2)}) collective-permute-start(bf16[3,32,1024]{2,1,0:T(8,128)(2,1)S(1)} %fusion.55), channel_id=1, source_target_pairs={{0,2},{1,3},{2,0},{3,1},{4,6},{5,7},{6,4},{7,5},{8,10},{9,11},{10,... | collective-permute-start | bytes 589832 | tf_op jit(solution)/shard_map/ppermute | solution.py:16
  122.1 40.8 %collective-permute-done.4 = bf16[3,32,1024]{2,1,0:T(8,128)(2,1)S(1)} collective-permute-done((bf16[3,32,1024]{2,1,0:T(8,128)(2,1)S(1)}, bf16[3,32,1024]{2,1,0:T(8,128)(2,1)S(1)}, u32[]{:S(2)}, u32[]{:S(2)}) %collective-permute-start.4) | collective-permute-done | bytes 196640 | tf_op jit(solution)/shard_map/ppermute | solution.py:16
  163.3 3.0 %collective-permute-start.5 = (bf16[3,32,1024]{2,1,0:T(8,128)(2,1)S(1)}, bf16[3,32,1024]{2,1,0:T(8,128)(2,1)S(1)}, u32[]{:S(2)}, u32[]{:S(2)}) collective-permute-start(bf16[3,32,1024]{2,1,0:T(8,128)(2,1)S(1)} %get-tuple-element.20), channel_id=1, source_target_pairs={{0,4},{1,5},{2,6},{3,7},{4,0},{5,1},{6,2},{7,3},{8,12},{9,13},{10,... | collective-permute-start | bytes 589832 | tf_op jit(solution)/shard_map/ppermute | solution.py:16
  166.2 5.1 %collective-permute-start.6 = (bf16[3,32,1024]{2,1,0:T(8,128)(2,1)S(1)}, bf16[3,32,1024]{2,1,0:T(8,128)(2,1)S(1)}, u32[]{:S(2)}, u32[]{:S(2)}) collective-permute-start(bf16[3,32,1024]{2,1,0:T(8,128)(2,1)S(1)} %get-tuple-element.20), channel_id=1, source_target_pairs={{0,8},{1,9},{2,10},{3,11},{4,12},{5,13},{6,14},{7,15},{8,0},{9,1},... | collective-permute-start | bytes 589832 | tf_op jit(solution)/shard_map/ppermute | solution.py:16
  171.3 2.4 collective-permute-start.7
  173.7 4.5 %collective-permute-done.6 = bf16[3,32,1024]{2,1,0:T(8,128)(2,1)S(1)} collective-permute-done((bf16[3,32,1024]{2,1,0:T(8,128)(2,1)S(1)}, bf16[3,32,1024]{2,1,0:T(8,128)(2,1)S(1)}, u32[]{:S(2)}, u32[]{:S(2)}) %collective-permute-start.6) | collective-permute-done | bytes 196640 | tf_op jit(solution)/shard_map/ppermute | solution.py:16
  178.2 4.1 %collective-permute-done.7 = bf16[3,32,1024]{2,1,0:T(8,128)(2,1)S(1)} collective-permute-done((bf16[3,32,1024]{2,1,0:T(8,128)(2,1)S(1)}, bf16[3,32,1024]{2,1,0:T(8,128)(2,1)S(1)}, u32[]{:S(2)}, u32[]{:S(2)}) %collective-permute-start.7) | collective-permute-done | bytes 196640 | tf_op jit(solution)/shard_map/ppermute | solution.py:16
  188.8 13.6 %collective-permute-done.9 = bf16[3,32,1024]{2,1,0:T(8,128)(2,1)} collective-permute-done((bf16[3,32,1024]{2,1,0:T(8,128)(2,1)}, bf16[3,32,1024]{2,1,0:T(8,128)(2,1)}, u32[]{:S(2)}, u32[]{:S(2)}) %collective-permute-start.9) | collective-permute-done | bytes 196640 | tf_op jit(solution)/shard_map/ppermute | solution.py:43
  203.3 19.5 %all-to-all-start.1 = ((bf16[64,4,448]{2,1,0:T(4,128)(2,1)}), bf16[64,4,448]{2,1,0:T(4,128)(2,1)S(1)}, u32[]{:S(2)}, u32[]{:S(2)}) async-start(bf16[64,4,448]{2,1,0:T(4,128)(2,1)} %reshape_reshape.7), calls=%async_computation.1 | async-start | bytes 524288 | tf_op jit(solution)/shard_map/all_to_all | solution.py:135
  223.8 2.0 collective-permute-start.10
  225.8 3.7 %collective-permute-start.11 = (bf16[3,32,1024]{2,1,0:T(8,128)(2,1)S(1)}, bf16[3,32,1024]{2,1,0:T(8,128)(2,1)S(1)}, u32[]{:S(2)}, u32[]{:S(2)}) collective-permute-start(bf16[3,32,1024]{2,1,0:T(8,128)(2,1)S(1)} %broadcast_select_fusion), channel_id=1, source_target_pairs={{0,8},{1,9},{2,10},{3,11},{4,12},{5,13},{6,14},{7,15},{8,0},{9,1},... | collective-permute-start | bytes 589832 | tf_op jit(solution)/shard_map/ppermute | solution.py:16
  229.6 4.7 %collective-permute-start.12 = (bf16[3,32,1024]{2,1,0:T(8,128)(2,1)S(1)}, bf16[3,32,1024]{2,1,0:T(8,128)(2,1)S(1)}, u32[]{:S(2)}, u32[]{:S(2)}) collective-permute-start(bf16[3,32,1024]{2,1,0:T(8,128)(2,1)S(1)} %broadcast_select_fusion), channel_id=1, source_target_pairs={{0,12},{1,13},{2,14},{3,15},{4,8},{5,9},{6,10},{7,11},{8,4},{9,5},... | collective-permute-start | bytes 589832 | tf_op jit(solution)/shard_map/ppermute | solution.py:16
  235.3 2.1 collective-permute-done.11
  237.3 4.1 %collective-permute-done.12 = bf16[3,32,1024]{2,1,0:T(8,128)(2,1)S(1)} collective-permute-done((bf16[3,32,1024]{2,1,0:T(8,128)(2,1)S(1)}, bf16[3,32,1024]{2,1,0:T(8,128)(2,1)S(1)}, u32[]{:S(2)}, u32[]{:S(2)}) %collective-permute-start.12) | collective-permute-done | bytes 196640 | tf_op jit(solution)/shard_map/ppermute | solution.py:16
  243.6 2.2 collective-permute-done.13
  249.3 9.2 %all-to-all-done.1 = bf16[64,4,448]{2,1,0:T(4,128)(2,1)S(1)} async-done(((bf16[64,4,448]{2,1,0:T(4,128)(2,1)}), bf16[64,4,448]{2,1,0:T(4,128)(2,1)S(1)}, u32[]{:S(2)}, u32[]{:S(2)}) %all-to-all-start.1) | async-done | bytes 229408 | tf_op jit(solution)/shard_map/all_to_all | solution.py:135
  (103 shorter events, 27.4 us)
Async XLA Ops:
  0.6 85.9 %copy-start = (bf16[1,1024,224]{1,2,0:T(8,128)(2,1)S(1)}, bf16[1,1024,224]{1,2,0:T(8,128)(2,1)}, u32[]{:S(2)}) copy-start(bf16[1,1024,224]{1,2,0:T(8,128)(2,1)} %param.13) | copy-start | bytes 1376260
  0.7 4.5 %copy-start.11 = (bf16[16,224]{1,0:T(8,128)(2,1)S(1)}, bf16[16,224]{1,0:T(8,128)(2,1)}, u32[]{:S(2)}) copy-start(bf16[16,224]{1,0:T(8,128)(2,1)} %param.15) | copy-start | bytes 21508
  6.9 78.3 %all-to-all-start = ((bf16[64,4,896]{2,1,0:T(4,128)(2,1)}), bf16[64,4,896]{2,1,0:T(4,128)(2,1)S(1)}, u32[]{:S(2)}, u32[]{:S(2)}) async-start(bf16[64,4,896]{2,1,0:T(4,128)(2,1)} %reshape.113), calls=%async_computation | async-start | bytes 917504 | tf_op jit(solution)/shard_map/all_to_all | solution.py:135
  87.2 5.3 %collective-permute-start = (f32[3,128,1024]{2,1,0:T(8,128)S(1)}, f32[3,128,1024]{2,1,0:T(8,128)S(1)}, u32[]{:S(2)}, u32[]{:S(2)}) collective-permute-start(f32[3,128,1024]{2,1,0:T(8,128)S(1)} %pad_maximum_fusion), channel_id=1, source_target_pairs={{0,1},{1,0},{2,3},{3,2},{4,5},{5,4},{6,7},{7,6},{8,9},{9,8},{10,11... | collective-permute-start | bytes 4718600 | tf_op jit(solution)/shard_map/ppermute | solution.py:16
  93.0 10.5 %collective-permute-start.1 = (bf16[3,32,1024]{2,1,0:T(8,128)(2,1)S(1)}, bf16[3,32,1024]{2,1,0:T(8,128)(2,1)S(1)}, u32[]{:S(2)}, u32[]{:S(2)}) collective-permute-start(bf16[3,32,1024]{2,1,0:T(8,128)(2,1)S(1)} %get-tuple-element.13), channel_id=1, source_target_pairs={{0,4},{1,5},{2,6},{3,7},{4,0},{5,1},{6,2},{7,3},{8,12},{9,13},{10,... | collective-permute-start | bytes 589832 | tf_op jit(solution)/shard_map/ppermute | solution.py:16
  95.7 10.3 %collective-permute-start.2 = (bf16[3,32,1024]{2,1,0:T(8,128)(2,1)S(1)}, bf16[3,32,1024]{2,1,0:T(8,128)(2,1)S(1)}, u32[]{:S(2)}, u32[]{:S(2)}) collective-permute-start(bf16[3,32,1024]{2,1,0:T(8,128)(2,1)S(1)} %get-tuple-element.15), channel_id=1, source_target_pairs={{0,8},{1,9},{2,10},{3,11},{4,12},{5,13},{6,14},{7,15},{8,0},{9,1},... | collective-permute-start | bytes 589832 | tf_op jit(solution)/shard_map/ppermute | solution.py:16
  98.8 11.4 %collective-permute-start.3 = (bf16[3,32,1024]{2,1,0:T(8,128)(2,1)S(1)}, bf16[3,32,1024]{2,1,0:T(8,128)(2,1)S(1)}, u32[]{:S(2)}, u32[]{:S(2)}) collective-permute-start(bf16[3,32,1024]{2,1,0:T(8,128)(2,1)S(1)} %get-tuple-element.14), channel_id=1, source_target_pairs={{0,12},{1,13},{2,14},{3,15},{4,8},{5,9},{6,10},{7,11},{8,4},{9,5},... | collective-permute-start | bytes 589832 | tf_op jit(solution)/shard_map/ppermute | solution.py:16
  110.3 52.7 %collective-permute-start.4 = (bf16[3,32,1024]{2,1,0:T(8,128)(2,1)S(1)}, bf16[3,32,1024]{2,1,0:T(8,128)(2,1)S(1)}, u32[]{:S(2)}, u32[]{:S(2)}) collective-permute-start(bf16[3,32,1024]{2,1,0:T(8,128)(2,1)S(1)} %fusion.55), channel_id=1, source_target_pairs={{0,2},{1,3},{2,0},{3,1},{4,6},{5,7},{6,4},{7,5},{8,10},{9,11},{10,... | collective-permute-start | bytes 589832 | tf_op jit(solution)/shard_map/ppermute | solution.py:16
  163.1 21.3 %copy-start.12 = (s32[32]{0:T(128)S(1)}, s32[32]{0:T(128)}, u32[]{:S(2)}) copy-start(s32[32]{0:T(128)} %param.11) | copy-start | bytes 388
  163.2 19.1 %copy-start.3 = (bf16[1,32,1024]{2,1,0:T(8,128)(2,1)}, bf16[1,32,1024]{2,1,0:T(8,128)(2,1)S(1)}, u32[]{:S(2)}) copy-start(bf16[1,32,1024]{2,1,0:T(8,128)(2,1)S(1)} %get-tuple-element.18) | copy-start | bytes 196612
  163.3 19.1 %copy-start.9 = (bf16[3,32,1024]{2,1,0:T(8,128)(2,1)}, bf16[3,32,1024]{2,1,0:T(8,128)(2,1)S(1)}, u32[]{:S(2)}) copy-start(bf16[3,32,1024]{2,1,0:T(8,128)(2,1)S(1)} %get-tuple-element.20) | copy-start | bytes 589828
  163.3 10.5 %collective-permute-start.5 = (bf16[3,32,1024]{2,1,0:T(8,128)(2,1)S(1)}, bf16[3,32,1024]{2,1,0:T(8,128)(2,1)S(1)}, u32[]{:S(2)}, u32[]{:S(2)}) collective-permute-start(bf16[3,32,1024]{2,1,0:T(8,128)(2,1)S(1)} %get-tuple-element.20), channel_id=1, source_target_pairs={{0,4},{1,5},{2,6},{3,7},{4,0},{5,1},{6,2},{7,3},{8,12},{9,13},{10,... | collective-permute-start | bytes 589832 | tf_op jit(solution)/shard_map/ppermute | solution.py:16
  166.2 12.0 %collective-permute-start.6 = (bf16[3,32,1024]{2,1,0:T(8,128)(2,1)S(1)}, bf16[3,32,1024]{2,1,0:T(8,128)(2,1)S(1)}, u32[]{:S(2)}, u32[]{:S(2)}) collective-permute-start(bf16[3,32,1024]{2,1,0:T(8,128)(2,1)S(1)} %get-tuple-element.20), channel_id=1, source_target_pairs={{0,8},{1,9},{2,10},{3,11},{4,12},{5,13},{6,14},{7,15},{8,0},{9,1},... | collective-permute-start | bytes 589832 | tf_op jit(solution)/shard_map/ppermute | solution.py:16
  171.3 11.0 %collective-permute-start.7 = (bf16[3,32,1024]{2,1,0:T(8,128)(2,1)S(1)}, bf16[3,32,1024]{2,1,0:T(8,128)(2,1)S(1)}, u32[]{:S(2)}, u32[]{:S(2)}) collective-permute-start(bf16[3,32,1024]{2,1,0:T(8,128)(2,1)S(1)} %get-tuple-element.20), channel_id=1, source_target_pairs={{0,12},{1,13},{2,14},{3,15},{4,8},{5,9},{6,10},{7,11},{8,4},{9,5},... | collective-permute-start | bytes 589832 | tf_op jit(solution)/shard_map/ppermute | solution.py:16
  182.5 5.1 %collective-permute-start.8 = (bf16[3,128,1024]{2,1,0:T(8,128)(2,1)S(1)}, bf16[3,128,1024]{2,1,0:T(8,128)(2,1)S(1)}, u32[]{:S(2)}, u32[]{:S(2)}) collective-permute-start(bf16[3,128,1024]{2,1,0:T(8,128)(2,1)S(1)} %bitcast.115), channel_id=1, source_target_pairs={{0,1},{1,0},{2,3},{3,2},{4,5},{5,4},{6,7},{7,6},{8,9},{9,8},{10,11... | collective-permute-start | bytes 2359304 | tf_op jit(solution)/shard_map/ppermute | solution.py:16
  185.7 16.7 %collective-permute-start.9 = (bf16[3,32,1024]{2,1,0:T(8,128)(2,1)}, bf16[3,32,1024]{2,1,0:T(8,128)(2,1)}, u32[]{:S(2)}, u32[]{:S(2)}) collective-permute-start(bf16[3,32,1024]{2,1,0:T(8,128)(2,1)} %copy-done.9), channel_id=1, source_target_pairs={{0,512},{1,515},{2,514},{3,513},{4,516},{5,519},{6,518},{7,517},{8... | collective-permute-start | bytes 589832 | tf_op jit(solution)/shard_map/ppermute | solution.py:43
  188.7 34.2 %copy-start.4 = (bf16[1,32,1024]{2,1,0:T(8,128)(2,1)S(1)}, bf16[1,32,1024]{2,1,0:T(8,128)(2,1)}, u32[]{:S(2)}) copy-start(bf16[1,32,1024]{2,1,0:T(8,128)(2,1)} %copy-done.3) | copy-start | bytes 196612
  203.3 55.2 %all-to-all-start.1 = ((bf16[64,4,448]{2,1,0:T(4,128)(2,1)}), bf16[64,4,448]{2,1,0:T(4,128)(2,1)S(1)}, u32[]{:S(2)}, u32[]{:S(2)}) async-start(bf16[64,4,448]{2,1,0:T(4,128)(2,1)} %reshape_reshape.7), calls=%async_computation.1 | async-start | bytes 524288 | tf_op jit(solution)/shard_map/all_to_all | solution.py:135
  223.8 11.4 %collective-permute-start.10 = (bf16[3,32,1024]{2,1,0:T(8,128)(2,1)S(1)}, bf16[3,32,1024]{2,1,0:T(8,128)(2,1)S(1)}, u32[]{:S(2)}, u32[]{:S(2)}) collective-permute-start(bf16[3,32,1024]{2,1,0:T(8,128)(2,1)S(1)} %broadcast_select_fusion), channel_id=1, source_target_pairs={{0,4},{1,5},{2,6},{3,7},{4,0},{5,1},{6,2},{7,3},{8,12},{9,13},{10,... | collective-permute-start | bytes 589832 | tf_op jit(solution)/shard_map/ppermute | solution.py:16
  225.8 11.5 %collective-permute-start.11 = (bf16[3,32,1024]{2,1,0:T(8,128)(2,1)S(1)}, bf16[3,32,1024]{2,1,0:T(8,128)(2,1)S(1)}, u32[]{:S(2)}, u32[]{:S(2)}) collective-permute-start(bf16[3,32,1024]{2,1,0:T(8,128)(2,1)S(1)} %broadcast_select_fusion), channel_id=1, source_target_pairs={{0,8},{1,9},{2,10},{3,11},{4,12},{5,13},{6,14},{7,15},{8,0},{9,1},... | collective-permute-start | bytes 589832 | tf_op jit(solution)/shard_map/ppermute | solution.py:16
  229.6 11.9 %collective-permute-start.12 = (bf16[3,32,1024]{2,1,0:T(8,128)(2,1)S(1)}, bf16[3,32,1024]{2,1,0:T(8,128)(2,1)S(1)}, u32[]{:S(2)}, u32[]{:S(2)}) collective-permute-start(bf16[3,32,1024]{2,1,0:T(8,128)(2,1)S(1)} %broadcast_select_fusion), channel_id=1, source_target_pairs={{0,12},{1,13},{2,14},{3,15},{4,8},{5,9},{6,10},{7,11},{8,4},{9,5},... | collective-permute-start | bytes 589832 | tf_op jit(solution)/shard_map/ppermute | solution.py:16
  241.6 4.2 %collective-permute-start.13 = (bf16[3,128,1024]{2,1,0:T(8,128)(2,1)S(1)}, bf16[3,128,1024]{2,1,0:T(8,128)(2,1)S(1)}, u32[]{:S(2)}, u32[]{:S(2)}) collective-permute-start(bf16[3,128,1024]{2,1,0:T(8,128)(2,1)S(1)} %bitcast.119), channel_id=1, source_target_pairs={{0,1},{1,0},{2,3},{3,2},{4,5},{5,4},{6,7},{7,6},{8,9},{9,8},{10,11... | collective-permute-start | bytes 2359304 | tf_op jit(solution)/shard_map/ppermute | solution.py:16
  248.1 10.5 %copy-start.6 = (pred[256,16]{1,0:T(32,128)(4,1)S(1)}, pred[256,16]{1,0:T(32,128)(4,1)}, u32[]{:S(2)}) copy-start(pred[256,16]{1,0:T(32,128)(4,1)} %copy-done.5) | copy-start | bytes 12292
  248.1 11.3 %copy-start.8 = (f32[64,16]{1,0:T(8,128)S(1)}, f32[64,16]{1,0:T(8,128)}, u32[]{:S(2)}) copy-start(f32[64,16]{1,0:T(8,128)} %copy-done.7) | copy-start | bytes 12292
  (5 other events, 10.6 us)
